TPU v7x, 256 devices: a whole 4x4x8 slice. The times are simulated.
256 devices in a mesh: expert: 64 (over x, z, core), hidden: 4 (over y).
Axes of the slice: x: 4, y: 4, z: 8, core: 2. Of those that a mesh axis runs over, the one named last changes fastest.
Arguments:
- tokens: bfloat16 [1024, 7168], P('expert', 'hidden'), may hold values from -6 to 6
- routes: int32 [1024, 8], P('expert'), may hold values from 0 to 63, as said below
- combine: float32 [1024, 8], P('expert'), may hold values from 0.05 to 0.5
- w_gate: bfloat16 [64, 7168, 1024], P('expert', None, 'hidden'), may hold values from -0.0625 to 0.0625
- w_up: bfloat16 [64, 7168, 1024], P('expert', None, 'hidden'), may hold values from -0.0625 to 0.0625
- w_down: bfloat16 [64, 1024, 7168], P('expert', 'hidden'), may hold values from -0.1875 to 0.1875
- cotangent: bfloat16 [1024, 7168], P('expert', 'hidden'), may hold values from -6 to 6
Outputs:
- output: bfloat16 [1024, 7168], P('expert', 'hidden')
- grad_tokens: bfloat16 [1024, 7168], P('expert', 'hidden')
Inputs may be any that keep to these rules, and one draw needn't show every extreme that they name: `routes`: each row names 8 different experts. In each aligned block of 16 rows (the rows of one device) no expert is named by more than 4 rows, and the same expert is named by exactly 4 rows in every block.
All inputs are finite; a program needn't handle non-finite values.
Results may differ from a plain program's by a relative error of at most 0.012.
Values may be sent and summed in bfloat16 or wider, within the bound.
No kernel may reach another device: no remote copies, remote signals or barrier semaphores. Data moves between devices by JAX's collectives and lax.ppermute only.
A program may use at most 128 MiB of HBM per device.

v0:
```python
import jax
import jax.numpy as jnp
from jax import lax
from jax.experimental import pallas as pl
from jax.experimental.pallas import tpu as pltpu
from jax.sharding import PartitionSpec as P


DIRECT = 384
CAP = 4


def gates_kernel(sums_ref, x_ref, far_ref, *refs):
    near_refs, (out_ref, relay_ref) = refs[:-2], refs[-2:]
    rows, cols = sums_ref.shape
    width = cols // 3
    depth = near_refs[0].shape[0]
    sums = sums_ref[...]
    for k, w_ref in enumerate(near_refs):
        x = x_ref[:, k * depth : (k + 1) * depth]
        sums = sums + jnp.dot(x, w_ref[...], preferred_element_type=jnp.float32)
    gate = sums[:, 0:width]
    up = sums[:, width : 2 * width]
    back = pltpu.roll(sums[:, 2 * width : 3 * width], rows - CAP, 0)
    first = lax.broadcasted_iota(jnp.int32, (rows, width), 0) % (2 * CAP) < CAP
    sig = jax.nn.sigmoid(gate)
    act = gate * sig
    zero = jnp.zeros_like(act)
    hidden = act * up
    grad_gate = back * up * sig * (1.0 + gate * (1.0 - sig))
    grad_up = back * act
    out = jnp.concatenate(
        [
            jnp.where(first, zero, pltpu.roll(grad_gate, CAP, 0)),
            jnp.where(first, zero, pltpu.roll(grad_up, CAP, 0)),
            jnp.where(first, hidden, zero),
        ],
        axis=1,
    ).astype(jnp.bfloat16)
    out_ref[...] = out
    relay_ref[...] = lax.dot_general(
        out, far_ref[...], (((1,), (1,)), ((), ())), preferred_element_type=jnp.float32
    ).astype(jnp.bfloat16)


def gates(sums, x, far, near):
    rows, cols = sums.shape
    depth = x.shape[1]
    reach = far.shape[0]
    block = 128
    return pl.pallas_call(
        gates_kernel,
        grid=(rows // block,),
        in_specs=[
            pl.BlockSpec((block, cols), lambda i: (i, 0)),
            pl.BlockSpec((block, depth), lambda i: (i, 0)),
            pl.BlockSpec(far.shape, lambda i: (0, 0)),
        ]
        + [pl.BlockSpec(w.shape, lambda i: (0, 0)) for w in near],
        out_specs=(
            pl.BlockSpec((block, cols), lambda i: (i, 0)),
            pl.BlockSpec((block, reach), lambda i: (i, 0)),
        ),
        out_shape=(
            jax.ShapeDtypeStruct((rows, cols), jnp.bfloat16),
            jax.ShapeDtypeStruct((rows, reach), jnp.bfloat16),
        ),
        cost_estimate=pl.CostEstimate(
            flops=2 * rows * cols * (depth + reach),
            bytes_accessed=rows * (cols * 6 + depth * 2 + reach * 2) + (depth + reach) * cols * 2,
            transcendentals=rows * cols // 3,
        ),
        name="gates",
    )(sums, x, far, *near)


def per_device(tokens, routes, combine, w_gate, w_up, w_down, cotangent):
    toks, slice_cols = tokens.shape
    sources = lax.axis_size("expert")
    parts = lax.axis_size("hidden")
    group = 2 * CAP
    rows = sources * group
    half = rows // 2
    me = lax.axis_index("hidden")
    f32, bf16 = jnp.float32, jnp.bfloat16

    def shift(v, k):
        return lax.ppermute(v, "hidden", [(i, (i + k) % parts) for i in range(parts)])

    def exchange(v):
        out = lax.all_to_all(
            v.reshape(sources, group, v.shape[1]), "expert", split_axis=0, concat_axis=0, tiled=True
        )
        return out.reshape(rows, v.shape[1])

    table = jnp.concatenate([tokens, cotangent], axis=0)
    direct = table[:, :DIRECT]
    direct_parts = [direct] + [shift(direct, parts - k) for k in range(1, parts)]

    row = lax.broadcasted_iota(jnp.int32, (toks, rows), 1)
    owner = row // group
    hit = routes[:, :, None] == owner[:, None, :]
    named = jnp.any(hit, axis=1)
    weight = jnp.sum(jnp.where(hit, combine[:, :, None], 0.0), axis=1)
    earlier = (
        lax.broadcasted_iota(jnp.int32, (toks, toks), 0)
        > lax.broadcasted_iota(jnp.int32, (toks, toks), 1)
    ).astype(bf16)
    rank = jnp.dot(earlier, named.astype(bf16), preferred_element_type=f32)
    placed = named & (rank.astype(jnp.int32) == row % CAP)
    is_token = row % group < CAP
    choose = jnp.concatenate([placed & is_token, placed & ~is_token], axis=0)
    select = choose.astype(bf16)

    def pack(values):
        return lax.dot_general(
            select, values, (((0,), (0,)), ((), ())), preferred_element_type=f32
        ).astype(bf16)

    w_gate, w_up, w_down = w_gate[0], w_up[0], w_down[0]

    def relative(k, lo, hi):
        start = ((me + k) % parts) * slice_cols + lo
        return jnp.concatenate(
            [
                lax.dynamic_slice_in_dim(w_gate, start, hi - lo, 0),
                lax.dynamic_slice_in_dim(w_up, start, hi - lo, 0),
                lax.dynamic_slice_in_dim(w_down, start, hi - lo, 1).T,
            ],
            axis=1,
        )

    w_near = [relative(k, 0, DIRECT) for k in range(parts)]
    w_far = [relative(k, DIRECT, slice_cols) for k in range(parts)]

    own = exchange(pack(table[:, DIRECT:]))
    packed_direct = pack(jnp.concatenate(direct_parts, axis=1))
    own, packed_direct, w_near, w_far = lax.optimization_barrier(
        (own, packed_direct, w_near, w_far)
    )
    top, bottom = own[:half], own[half:]
    l_top = shift(top, 1)
    r_bottom = shift(bottom, -1)
    arrived_direct = exchange(packed_direct)
    top, bottom, l_top, r_bottom = lax.optimization_barrier((top, bottom, l_top, r_bottom))
    o_top = shift(l_top, 1)
    o_bottom = shift(r_bottom, -1)
    l_bottom = shift(bottom, 1)
    r_top = shift(top, -1)
    sums = jnp.dot(own, w_far[0], preferred_element_type=f32)
    for k, v in (
        (2, jnp.concatenate([o_top, o_bottom], axis=0)),
        (3, jnp.concatenate([l_top, l_bottom], axis=0)),
        (1, jnp.concatenate([r_top, r_bottom], axis=0)),
    ):
        sums = sums + jnp.dot(v, w_far[k], preferred_element_type=f32)
    grads, relay = gates(sums, arrived_direct, w_far[2], w_near)

    def product(w, lo, hi):
        return lax.dot_general(
            grads[lo:hi], w, (((1,), (1,)), ((), ())), preferred_element_type=f32
        )

    spread = choose * jnp.concatenate([weight, weight], axis=0)
    coarse = lax.reduce_precision(spread, 8, 7)
    fine = (spread - coarse).astype(bf16)
    coarse = coarse.astype(bf16)

    def mix(back):
        return jnp.dot(coarse, back, preferred_element_type=f32) + jnp.dot(
            fine, back, preferred_element_type=f32
        )

    o_top = shift(relay[:half], 1)
    o_bottom = shift(relay[half:], -1)
    back_direct = exchange(
        jnp.concatenate([product(w, 0, rows) for w in w_near], axis=1).astype(bf16)
    )
    p_bottom = product(w_far[1], half, rows).astype(bf16)
    p_top = product(w_far[3], 0, half).astype(bf16)
    o_top, o_bottom, p_bottom, p_top = lax.optimization_barrier((o_top, o_bottom, p_bottom, p_top))
    l_top = shift((product(w_far[1], 0, half) + o_top.astype(f32)).astype(bf16), 1)
    r_bottom = shift((product(w_far[3], half, rows) + o_bottom.astype(f32)).astype(bf16), -1)
    l_bottom = shift(p_bottom, 1)
    r_top = shift(p_top, -1)
    total = (
        product(w_far[0], 0, rows)
        + jnp.concatenate([l_top, l_bottom], axis=0).astype(f32)
        + jnp.concatenate([r_top, r_bottom], axis=0).astype(f32)
    ).astype(bf16)
    total, back_direct = lax.optimization_barrier((total, back_direct))
    back_far = exchange(total)

    mixed = mix(back_direct)
    near = mixed[:, :DIRECT]
    for k in range(1, parts):
        near = near + shift(mixed[:, k * DIRECT : (k + 1) * DIRECT].astype(bf16), k).astype(f32)
    result = jnp.concatenate([near.astype(bf16), mix(back_far).astype(bf16)], axis=1)
    return result[:toks], result[toks:]


def solution(mesh):
    return jax.shard_map(
        per_device,
        mesh=mesh,
        in_specs=(
            P("expert", "hidden"),
            P("expert", None),
            P("expert", None),
            P("expert", None, "hidden"),
            P("expert", None, "hidden"),
            P("expert", "hidden", None),
            P("expert", "hidden"),
        ),
        out_specs=(P("expert", "hidden"), P("expert", "hidden")),
        check_vma=False,
    )
```

profile of v0, /device:TPU:1, one launch (start us, length us, event | category | flops | bytes accessed | tf_op | source)
XLA Modules:
  0.0 264.3 jit_solution(6033474713482270254)
XLA Ops:
  4.4 2.6 collective-permute-start.1
  11.4 13.2 %all-to-all-start = ((bf16[64,8,1408]{2,1,0:T(8,128)(2,1)}), bf16[64,8,1408]{2,1,0:T(8,128)(2,1)}, u32[]{:S(2)}, u32[]{:S(2)}) async-start(bf16[64,8,1408]{2,1,0:T(8,128)(2,1)} %fusion), calls=%async_computation | async-start | bytes 2883584 | tf_op jit(solution)/shard_map/all_to_all | solution.py:91
  46.3 2.5 convolution_convert_fusion
  48.8 12.6 %all-to-all-done = bf16[64,8,1408]{2,1,0:T(8,128)(2,1)} async-done(((bf16[64,8,1408]{2,1,0:T(8,128)(2,1)}), bf16[64,8,1408]{2,1,0:T(8,128)(2,1)}, u32[]{:S(2)}, u32[]{:S(2)}) %all-to-all-start) | async-done | bytes 1441824 | tf_op jit(solution)/shard_map/all_to_all | solution.py:91
  61.4 6.3 %all-to-all-start.1 = ((bf16[64,8,1536]{2,1,0:T(8,128)(2,1)}), bf16[64,8,1536]{2,1,0:T(8,128)(2,1)}, u32[]{:S(2)}, u32[]{:S(2)}) async-start(bf16[64,8,1536]{2,1,0:T(8,128)(2,1)} %bitcast.100), calls=%async_computation.1 | async-start | bytes 3145728 | tf_op jit(solution)/shard_map/all_to_all | solution.py:91
  70.9 15.8 %collective-permute-done.4 = bf16[256,1408]{1,0:T(8,128)(2,1)S(1)} collective-permute-done((bf16[256,1408]{1,0:T(8,128)(2,1)S(1)}, bf16[256,1408]{1,0:T(8,128)(2,1)S(1)}, u32[]{:S(2)}, u32[]{:S(2)}) %collective-permute-start.4) | collective-permute-done | bytes 720928 | tf_op jit(solution)/shard_map/ppermute | solution.py:88
  88.0 2.7 %collective-permute-start.8 = (bf16[256,1408]{1,0:T(8,128)(2,1)S(1)}, bf16[256,1408]{1,0:T(8,128)(2,1)S(1)}, u32[]{:S(2)}, u32[]{:S(2)}) collective-permute-start(bf16[256,1408]{1,0:T(8,128)(2,1)S(1)} %get-tuple-element.31), channel_id=1, source_target_pairs={{0,3},{1,0},{2,1},{3,2},{4,7},{5,4},{6,5},{7,6},{8,11},{9,8},{10,9... | collective-permute-start | bytes 2162696 | tf_op jit(solution)/shard_map/ppermute | solution.py:88
  90.7 2.7 %collective-permute-start.6 = (bf16[256,1408]{1,0:T(8,128)(2,1)S(1)}, bf16[256,1408]{1,0:T(8,128)(2,1)S(1)}, u32[]{:S(2)}, u32[]{:S(2)}) collective-permute-start(bf16[256,1408]{1,0:T(8,128)(2,1)S(1)} %collective-permute-done.4), channel_id=1, source_target_pairs={{0,3},{1,0},{2,1},{3,2},{4,7},{5,4},{6,5},{7,6},{8,11},{9,8},{10,9... | collective-permute-start | bytes 2162696 | tf_op jit(solution)/shard_map/ppermute | solution.py:88
  93.4 2.7 %fusion.77 = f32[512,768]{1,0:T(8,128)S(1)} fusion(bf16[512,1408]{1,0:T(8,128)(2,1)} %bitcast.1, bf16[1408,768]{1,0:T(8,128)(2,1)S(1)} %copy-done.8), kind=kOutput, calls=%fused_computation.141 | convolution fusion | flops 1107296256 | bytes 5177344 | tf_op jit(solution)/shard_map/dot_general | solution.py:150
  96.1 9.6 %collective-permute-done.7 = bf16[256,1408]{1,0:T(8,128)(2,1)S(1)} collective-permute-done((bf16[256,1408]{1,0:T(8,128)(2,1)S(1)}, bf16[256,1408]{1,0:T(8,128)(2,1)S(1)}, u32[]{:S(2)}, u32[]{:S(2)}) %collective-permute-start.7) | collective-permute-done | bytes 720928 | tf_op jit(solution)/shard_map/ppermute | solution.py:88
  107.2 13.9 %collective-permute-done.5 = bf16[256,1408]{1,0:T(8,128)(2,1)S(1)} collective-permute-done((bf16[256,1408]{1,0:T(8,128)(2,1)S(1)}, bf16[256,1408]{1,0:T(8,128)(2,1)S(1)}, u32[]{:S(2)}, u32[]{:S(2)}) %collective-permute-start.5) | collective-permute-done | bytes 720928 | tf_op jit(solution)/shard_map/ppermute | solution.py:88
  122.5 2.6 add_add_fusion.sums_ref
  125.1 9.9 %gates.1 = (bf16[512,768]{1,0:T(8,128)(2,1)}, bf16[512,1408]{1,0:T(8,128)(2,1)}) custom-call(f32[512,768]{1,0:T(8,128)} %add_add_fusion.sums_ref, bf16[512,1536]{1,0:T(8,128)(2,1)} %bitcast.35.x_ref, bf16[1408,768]{1,0:T(8,128)(2,1)} %pad_maximum_fusion.2.far_ref, bf16[384,768]{1,0:T(8,128)(2,1)} %pad_maximum_fusion.5.refs_0_, ...), custom_call_target="tpu_custom_call" | custom-call | flops 2315255808 | bytes 9895936 | tf_op jit(solution)/shard_map/gates/pallas_call | solution.py:51
  144.4 12.2 %all-to-all-start.2 = ((bf16[64,8,1536]{2,1,0:T(8,128)(2,1)}), bf16[64,8,1536]{2,1,0:T(8,128)(2,1)S(1)}, u32[]{:S(2)}, u32[]{:S(2)}) async-start(bf16[64,8,1536]{2,1,0:T(8,128)(2,1)} %pad_maximum_fusion.4), calls=%async_computation.2 | async-start | bytes 3145728 | tf_op jit(solution)/shard_map/all_to_all | solution.py:91
  156.6 2.8 %collective-permute-start.10 = (bf16[256,1408]{1,0:T(8,128)(2,1)}, bf16[256,1408]{1,0:T(8,128)(2,1)S(1)}, u32[]{:S(2)}, u32[]{:S(2)}) collective-permute-start(bf16[256,1408]{1,0:T(8,128)(2,1)} %get-tuple-element.70), channel_id=1, source_target_pairs={{0,3},{1,0},{2,1},{3,2},{4,7},{5,4},{6,5},{7,6},{8,11},{9,8},{10,9... | collective-permute-start | bytes 2162696 | tf_op jit(solution)/shard_map/ppermute | solution.py:88
  164.2 10.5 %collective-permute-done.10 = bf16[256,1408]{1,0:T(8,128)(2,1)S(1)} collective-permute-done((bf16[256,1408]{1,0:T(8,128)(2,1)}, bf16[256,1408]{1,0:T(8,128)(2,1)S(1)}, u32[]{:S(2)}, u32[]{:S(2)}) %collective-permute-start.10) | collective-permute-done | bytes 720928 | tf_op jit(solution)/shard_map/ppermute | solution.py:88
  174.7 3.0 %collective-permute-done.9 = bf16[256,1408]{1,0:T(8,128)(2,1)S(1)} collective-permute-done((bf16[256,1408]{1,0:T(8,128)(2,1)}, bf16[256,1408]{1,0:T(8,128)(2,1)S(1)}, u32[]{:S(2)}, u32[]{:S(2)}) %collective-permute-start.9) | collective-permute-done | bytes 720928 | tf_op jit(solution)/shard_map/ppermute | solution.py:88
  178.1 2.7 %collective-permute-start.13 = (bf16[256,1408]{1,0:T(8,128)(2,1)S(1)}, bf16[256,1408]{1,0:T(8,128)(2,1)S(1)}, u32[]{:S(2)}, u32[]{:S(2)}) collective-permute-start(bf16[256,1408]{1,0:T(8,128)(2,1)S(1)} %copy-done.22), channel_id=1, source_target_pairs={{0,3},{1,0},{2,1},{3,2},{4,7},{5,4},{6,5},{7,6},{8,11},{9,8},{10,9... | collective-permute-start | bytes 2162696 | tf_op jit(solution)/shard_map/ppermute | solution.py:88
  182.3 13.0 %collective-permute-done.11 = bf16[256,1408]{1,0:T(8,128)(2,1)S(1)} collective-permute-done((bf16[256,1408]{1,0:T(8,128)(2,1)S(1)}, bf16[256,1408]{1,0:T(8,128)(2,1)S(1)}, u32[]{:S(2)}, u32[]{:S(2)}) %collective-permute-start.11) | collective-permute-done | bytes 720928 | tf_op jit(solution)/shard_map/ppermute | solution.py:88
  195.3 15.4 %collective-permute-done.12 = bf16[256,1408]{1,0:T(8,128)(2,1)S(1)} collective-permute-done((bf16[256,1408]{1,0:T(8,128)(2,1)S(1)}, bf16[256,1408]{1,0:T(8,128)(2,1)S(1)}, u32[]{:S(2)}, u32[]{:S(2)}) %collective-permute-start.12) | collective-permute-done | bytes 720928 | tf_op jit(solution)/shard_map/ppermute | solution.py:88
  210.7 2.6 add_convert_fusion
  213.4 12.6 %all-to-all-start.3 = ((bf16[64,8,1408]{2,1,0:T(8,128)(2,1)}), bf16[64,8,1408]{2,1,0:T(8,128)(2,1)S(1)}, u32[]{:S(2)}, u32[]{:S(2)}) async-start(bf16[64,8,1408]{2,1,0:T(8,128)(2,1)} %bitcast.105), calls=%async_computation.3 | async-start | bytes 2883584 | tf_op jit(solution)/shard_map/all_to_all | solution.py:91
  231.4 3.1 %collective-permute-done.16 = bf16[32,384]{1,0:T(8,128)(2,1)S(1)} collective-permute-done((bf16[32,384]{1,0:T(8,128)(2,1)S(1)}, bf16[32,384]{1,0:T(8,128)(2,1)S(1)}, u32[]{:S(2)}, u32[]{:S(2)}) %collective-permute-start.16) | collective-permute-done | bytes 24608 | tf_op jit(solution)/shard_map/ppermute | solution.py:88
  234.4 28.5 %all-to-all-done.3 = bf16[64,8,1408]{2,1,0:T(8,128)(2,1)S(1)} async-done(((bf16[64,8,1408]{2,1,0:T(8,128)(2,1)}), bf16[64,8,1408]{2,1,0:T(8,128)(2,1)S(1)}, u32[]{:S(2)}, u32[]{:S(2)}) %all-to-all-start.3) | async-done | bytes 1441824 | tf_op jit(solution)/shard_map/all_to_all | solution.py:91
  (128 shorter events, 59.6 us)
Async XLA Ops:
  2.3 44.0 %collective-permute-start.2 = (bf16[32,384]{1,0:T(8,128)(2,1)S(1)}, bf16[32,384]{1,0:T(8,128)(2,1)S(1)}, u32[]{:S(2)}, u32[]{:S(2)}) collective-permute-start(bf16[32,384]{1,0:T(8,128)(2,1)S(1)} %slice.62), channel_id=1, source_target_pairs={{0,1},{1,2},{2,3},{3,0},{4,5},{5,6},{6,7},{7,4},{8,9},{9,10},{10,1... | collective-permute-start | bytes 73736 | tf_op jit(solution)/shard_map/ppermute | solution.py:88
  4.4 41.9 %collective-permute-start.1 = (bf16[32,384]{1,0:T(8,128)(2,1)S(1)}, bf16[32,384]{1,0:T(8,128)(2,1)}, u32[]{:S(2)}, u32[]{:S(2)}) collective-permute-start(bf16[32,384]{1,0:T(8,128)(2,1)S(1)} %slice.62), channel_id=1, source_target_pairs={{0,2},{1,3},{2,0},{3,1},{4,6},{5,7},{6,4},{7,5},{8,10},{9,11},{10,... | collective-permute-start | bytes 73736 | tf_op jit(solution)/shard_map/ppermute | solution.py:88
  7.0 39.3 %collective-permute-start = (bf16[32,384]{1,0:T(8,128)(2,1)S(1)}, bf16[32,384]{1,0:T(8,128)(2,1)}, u32[]{:S(2)}, u32[]{:S(2)}) collective-permute-start(bf16[32,384]{1,0:T(8,128)(2,1)S(1)} %slice.62), channel_id=1, source_target_pairs={{0,3},{1,0},{2,1},{3,2},{4,7},{5,4},{6,5},{7,6},{8,11},{9,8},{10,9... | collective-permute-start | bytes 73736 | tf_op jit(solution)/shard_map/ppermute | solution.py:88
  11.4 50.1 %all-to-all-start = ((bf16[64,8,1408]{2,1,0:T(8,128)(2,1)}), bf16[64,8,1408]{2,1,0:T(8,128)(2,1)}, u32[]{:S(2)}, u32[]{:S(2)}) async-start(bf16[64,8,1408]{2,1,0:T(8,128)(2,1)} %fusion), calls=%async_computation | async-start | bytes 2883584 | tf_op jit(solution)/shard_map/all_to_all | solution.py:91
  39.7 100.3 %copy-start = (bf16[1408,768]{1,0:T(8,128)(2,1)}, bf16[1408,768]{1,0:T(8,128)(2,1)S(1)}, u32[]{:S(2)}) copy-start(bf16[1408,768]{1,0:T(8,128)(2,1)S(1)} %pad_maximum_fusion.3) | copy-start | bytes 6488068
  61.4 63.7 %all-to-all-start.1 = ((bf16[64,8,1536]{2,1,0:T(8,128)(2,1)}), bf16[64,8,1536]{2,1,0:T(8,128)(2,1)}, u32[]{:S(2)}, u32[]{:S(2)}) async-start(bf16[64,8,1536]{2,1,0:T(8,128)(2,1)} %bitcast.100), calls=%async_computation.1 | async-start | bytes 3145728 | tf_op jit(solution)/shard_map/all_to_all | solution.py:91
  69.4 17.4 %collective-permute-start.4 = (bf16[256,1408]{1,0:T(8,128)(2,1)S(1)}, bf16[256,1408]{1,0:T(8,128)(2,1)S(1)}, u32[]{:S(2)}, u32[]{:S(2)}) collective-permute-start(bf16[256,1408]{1,0:T(8,128)(2,1)S(1)} %get-tuple-element.29), channel_id=1, source_target_pairs={{0,3},{1,0},{2,1},{3,2},{4,7},{5,4},{6,5},{7,6},{8,11},{9,8},{10,9... | collective-permute-start | bytes 2162696 | tf_op jit(solution)/shard_map/ppermute | solution.py:88
  69.5 18.6 %collective-permute-start.3 = (bf16[256,1408]{1,0:T(8,128)(2,1)S(1)}, bf16[256,1408]{1,0:T(8,128)(2,1)S(1)}, u32[]{:S(2)}, u32[]{:S(2)}) collective-permute-start(bf16[256,1408]{1,0:T(8,128)(2,1)S(1)} %get-tuple-element.31), channel_id=1, source_target_pairs={{0,1},{1,2},{2,3},{3,0},{4,5},{5,6},{6,7},{7,4},{8,9},{9,10},{10,1... | collective-permute-start | bytes 2162696 | tf_op jit(solution)/shard_map/ppermute | solution.py:88
  88.0 17.7 %collective-permute-start.7 = (bf16[256,1408]{1,0:T(8,128)(2,1)S(1)}, bf16[256,1408]{1,0:T(8,128)(2,1)S(1)}, u32[]{:S(2)}, u32[]{:S(2)}) collective-permute-start(bf16[256,1408]{1,0:T(8,128)(2,1)S(1)} %get-tuple-element.29), channel_id=1, source_target_pairs={{0,1},{1,2},{2,3},{3,0},{4,5},{5,6},{6,7},{7,4},{8,9},{9,10},{10,1... | collective-permute-start | bytes 2162696 | tf_op jit(solution)/shard_map/ppermute | solution.py:88
  88.0 34.5 %collective-permute-start.8 = (bf16[256,1408]{1,0:T(8,128)(2,1)S(1)}, bf16[256,1408]{1,0:T(8,128)(2,1)S(1)}, u32[]{:S(2)}, u32[]{:S(2)}) collective-permute-start(bf16[256,1408]{1,0:T(8,128)(2,1)S(1)} %get-tuple-element.31), channel_id=1, source_target_pairs={{0,3},{1,0},{2,1},{3,2},{4,7},{5,4},{6,5},{7,6},{8,11},{9,8},{10,9... | collective-permute-start | bytes 2162696 | tf_op jit(solution)/shard_map/ppermute | solution.py:88
  90.7 30.4 %collective-permute-start.5 = (bf16[256,1408]{1,0:T(8,128)(2,1)S(1)}, bf16[256,1408]{1,0:T(8,128)(2,1)S(1)}, u32[]{:S(2)}, u32[]{:S(2)}) collective-permute-start(bf16[256,1408]{1,0:T(8,128)(2,1)S(1)} %collective-permute-done.3), channel_id=1, source_target_pairs={{0,1},{1,2},{2,3},{3,0},{4,5},{5,6},{6,7},{7,4},{8,9},{9,10},{10,1... | collective-permute-start | bytes 2162696 | tf_op jit(solution)/shard_map/ppermute | solution.py:88
  90.7 30.4 %collective-permute-start.6 = (bf16[256,1408]{1,0:T(8,128)(2,1)S(1)}, bf16[256,1408]{1,0:T(8,128)(2,1)S(1)}, u32[]{:S(2)}, u32[]{:S(2)}) collective-permute-start(bf16[256,1408]{1,0:T(8,128)(2,1)S(1)} %collective-permute-done.4), channel_id=1, source_target_pairs={{0,3},{1,0},{2,1},{3,2},{4,7},{5,4},{6,5},{7,6},{8,11},{9,8},{10,9... | collective-permute-start | bytes 2162696 | tf_op jit(solution)/shard_map/ppermute | solution.py:88
  144.4 69.0 %all-to-all-start.2 = ((bf16[64,8,1536]{2,1,0:T(8,128)(2,1)}), bf16[64,8,1536]{2,1,0:T(8,128)(2,1)S(1)}, u32[]{:S(2)}, u32[]{:S(2)}) async-start(bf16[64,8,1536]{2,1,0:T(8,128)(2,1)} %pad_maximum_fusion.4), calls=%async_computation.2 | async-start | bytes 3145728 | tf_op jit(solution)/shard_map/all_to_all | solution.py:91
  156.6 18.1 %collective-permute-start.10 = (bf16[256,1408]{1,0:T(8,128)(2,1)}, bf16[256,1408]{1,0:T(8,128)(2,1)S(1)}, u32[]{:S(2)}, u32[]{:S(2)}) collective-permute-start(bf16[256,1408]{1,0:T(8,128)(2,1)} %get-tuple-element.70), channel_id=1, source_target_pairs={{0,3},{1,0},{2,1},{3,2},{4,7},{5,4},{6,5},{7,6},{8,11},{9,8},{10,9... | collective-permute-start | bytes 2162696 | tf_op jit(solution)/shard_map/ppermute | solution.py:88
  159.3 18.4 %collective-permute-start.9 = (bf16[256,1408]{1,0:T(8,128)(2,1)}, bf16[256,1408]{1,0:T(8,128)(2,1)S(1)}, u32[]{:S(2)}, u32[]{:S(2)}) collective-permute-start(bf16[256,1408]{1,0:T(8,128)(2,1)} %get-tuple-element.71), channel_id=1, source_target_pairs={{0,1},{1,2},{2,3},{3,0},{4,5},{5,6},{6,7},{7,4},{8,9},{9,10},{10,1... | collective-permute-start | bytes 2162696 | tf_op jit(solution)/shard_map/ppermute | solution.py:88
  177.9 32.9 %copy-start.9 = (bf16[1408,768]{1,0:T(8,128)(2,1)S(1)}, bf16[1408,768]{1,0:T(8,128)(2,1)}, u32[]{:S(2)}) copy-start(bf16[1408,768]{1,0:T(8,128)(2,1)} %pad_maximum_fusion) | copy-start | bytes 6488068
  177.9 17.4 %collective-permute-start.11 = (bf16[256,1408]{1,0:T(8,128)(2,1)S(1)}, bf16[256,1408]{1,0:T(8,128)(2,1)S(1)}, u32[]{:S(2)}, u32[]{:S(2)}) collective-permute-start(bf16[256,1408]{1,0:T(8,128)(2,1)S(1)} %add_convert_fusion.2), channel_id=1, source_target_pairs={{0,1},{1,2},{2,3},{3,0},{4,5},{5,6},{6,7},{7,4},{8,9},{9,10},{10,1... | collective-permute-start | bytes 2162696 | tf_op jit(solution)/shard_map/ppermute | solution.py:88
  178.0 32.8 %collective-permute-start.12 = (bf16[256,1408]{1,0:T(8,128)(2,1)S(1)}, bf16[256,1408]{1,0:T(8,128)(2,1)S(1)}, u32[]{:S(2)}, u32[]{:S(2)}) collective-permute-start(bf16[256,1408]{1,0:T(8,128)(2,1)S(1)} %convolution_convert_fusion.3), channel_id=1, source_target_pairs={{0,1},{1,2},{2,3},{3,0},{4,5},{5,6},{6,7},{7,4},{8,9},{9,10},{10,1... | collective-permute-start | bytes 2162696 | tf_op jit(solution)/shard_map/ppermute | solution.py:88
  178.1 32.7 %collective-permute-start.13 = (bf16[256,1408]{1,0:T(8,128)(2,1)S(1)}, bf16[256,1408]{1,0:T(8,128)(2,1)S(1)}, u32[]{:S(2)}, u32[]{:S(2)}) collective-permute-start(bf16[256,1408]{1,0:T(8,128)(2,1)S(1)} %copy-done.22), channel_id=1, source_target_pairs={{0,3},{1,0},{2,1},{3,2},{4,7},{5,4},{6,5},{7,6},{8,11},{9,8},{10,9... | collective-permute-start | bytes 2162696 | tf_op jit(solution)/shard_map/ppermute | solution.py:88
  180.8 29.9 %collective-permute-start.14 = (bf16[256,1408]{1,0:T(8,128)(2,1)S(1)}, bf16[256,1408]{1,0:T(8,128)(2,1)S(1)}, u32[]{:S(2)}, u32[]{:S(2)}) collective-permute-start(bf16[256,1408]{1,0:T(8,128)(2,1)S(1)} %add_convert_fusion.1), channel_id=1, source_target_pairs={{0,3},{1,0},{2,1},{3,2},{4,7},{5,4},{6,5},{7,6},{8,11},{9,8},{10,9... | collective-permute-start | bytes 2162696 | tf_op jit(solution)/shard_map/ppermute | solution.py:88
  213.4 49.6 %all-to-all-start.3 = ((bf16[64,8,1408]{2,1,0:T(8,128)(2,1)}), bf16[64,8,1408]{2,1,0:T(8,128)(2,1)S(1)}, u32[]{:S(2)}, u32[]{:S(2)}) async-start(bf16[64,8,1408]{2,1,0:T(8,128)(2,1)} %bitcast.105), calls=%async_computation.3 | async-start | bytes 2883584 | tf_op jit(solution)/shard_map/all_to_all | solution.py:91
  227.0 4.3 %collective-permute-start.15 = (bf16[32,384]{1,0:T(8,128)(2,1)S(1)}, bf16[32,384]{1,0:T(8,128)(2,1)S(1)}, u32[]{:S(2)}, u32[]{:S(2)}) collective-permute-start(bf16[32,384]{1,0:T(8,128)(2,1)S(1)} %get-tuple-element.76), channel_id=1, source_target_pairs={{0,1},{1,2},{2,3},{3,0},{4,5},{5,6},{6,7},{7,4},{8,9},{9,10},{10,1... | collective-permute-start | bytes 73736 | tf_op jit(solution)/shard_map/ppermute | solution.py:88
  227.9 3.4 %collective-permute-start.17 = (bf16[32,384]{1,0:T(8,128)(2,1)S(1)}, bf16[32,384]{1,0:T(8,128)(2,1)S(1)}, u32[]{:S(2)}, u32[]{:S(2)}) collective-permute-start(bf16[32,384]{1,0:T(8,128)(2,1)S(1)} %get-tuple-element.77), channel_id=1, source_target_pairs={{0,3},{1,0},{2,1},{3,2},{4,7},{5,4},{6,5},{7,6},{8,11},{9,8},{10,9... | collective-permute-start | bytes 73736 | tf_op jit(solution)/shard_map/ppermute | solution.py:88
  229.9 4.5 %collective-permute-start.16 = (bf16[32,384]{1,0:T(8,128)(2,1)S(1)}, bf16[32,384]{1,0:T(8,128)(2,1)S(1)}, u32[]{:S(2)}, u32[]{:S(2)}) collective-permute-start(bf16[32,384]{1,0:T(8,128)(2,1)S(1)} %get-tuple-element.78), channel_id=1, source_target_pairs={{0,2},{1,3},{2,0},{3,1},{4,6},{5,7},{6,4},{7,5},{8,10},{9,11},{10,... | collective-permute-start | bytes 73736 | tf_op jit(solution)/shard_map/ppermute | solution.py:88
  (21 other events, 160.9 us)
where the time goes:
time: 265 us; the launch traced here: 264 us
  waiting for transfers between devices  127 us (48%)
  starting transfers between devices  68.2 us (26%)
  matrix products  27.3 us (10%)
  local copies, waits for them, and re-layouts  19.9 us (8%)
  other arithmetic  10.9 us (4%)
  Pallas kernels  9.92 us (4%)
    ppermute x18, waiting for transfers between devices, shift(): lax.ppermute(v, 'hidden', [(i, (i + k) % parts) for i in range(parts)])  85.8 us
    all_to_all x4, starting transfers between devices, exchange(): lax.all_to_all(v.reshape(sources, group, v.shape[1]), 'expert', split_axi...  44.3 us
    all_to_all x4, waiting for transfers between devices, exchange(): lax.all_to_all(v.reshape(sources, group, v.shape[1]), 'expert', split_axi...  41.1 us
    ppermute x18, starting transfers between devices, shift(): lax.ppermute(v, 'hidden', [(i, (i + k) % parts) for i in range(parts)])  23.9 us
    dot_general x9, matrix products, product(): lax.dot_general(grads[lo:hi], w, (((1,), (1,)), ((), ())), preferred_elem...  13.3 us
    pallas_call x1, Pallas kernels, gates(): pl.pallas_call(gates_kernel, grid=(rows // block,), in_specs=[pl.BlockSpe...  9.92 us
    dynamic_slice x10, local copies, waits for them, and re-layouts, relative(): lax.dynamic_slice_in_dim(w_down, start, hi - lo, 1)  8.32 us
    concatenate x8, other arithmetic, relative(): jnp.concatenate([lax.dynamic_slice_in_dim(w_gate, start, hi - lo, 0), lax...  8.21 us
  transfers between devices with their start and end apart: 22, of which 12 were waited for; matrix products, arithmetic and copies ran while one was open for 16% of the time, Pallas kernels for 0%

commit v1 on v0

v1 whole, which is shorter than its diff:
```python
import jax
import jax.numpy as jnp
from jax import lax
from jax.experimental import pallas as pl
from jax.experimental.pallas import tpu as pltpu
from jax.sharding import PartitionSpec as P


DIRECT = 384
CAP = 4
LANES = 128
MIB = 1 << 20
F32, BF16 = jnp.float32, jnp.bfloat16
ANY = pl.BlockSpec(memory_space=pl.ANY)
HBM = pl.BlockSpec(memory_space=pltpu.HBM)
SMEM = pl.BlockSpec(memory_space=pltpu.SMEM)
VMEM = pl.BlockSpec(memory_space=pltpu.VMEM)


def dot(a, b):
    return jnp.dot(a, b, preferred_element_type=F32)


def dot_t(a, b):
    return lax.dot_general(a, b, (((1,), (1,)), ((), ())), preferred_element_type=F32)


class Plan:
    def __init__(self, parts, depth, width):
        self.parts, self.depth, self.width = parts, depth, width
        self.slice = depth // parts
        self.far = self.slice - DIRECT

    def weight_scratch(self, reach):
        w = self.width
        return [pltpu.VMEM((reach, w), BF16), pltpu.VMEM((reach, w), BF16), pltpu.VMEM((w, reach), BF16)]

    def copies(self, me_ref, k, lo, reach, hbm, bufs, sems, at=0):
        start = pl.multiple_of(((me_ref[0] + k) % self.parts) * self.slice + lo, LANES)
        here, there = pl.ds(at, reach), pl.ds(start, reach)
        return [
            pltpu.make_async_copy(hbm[0].at[there, :], bufs[0].at[here, :], sems.at[0]),
            pltpu.make_async_copy(hbm[1].at[there, :], bufs[1].at[here, :], sems.at[1]),
            pltpu.make_async_copy(hbm[2].at[:, there], bufs[2].at[:, here], sems.at[2]),
        ]


def run(copies):
    for c in copies:
        c.start()
    return copies


def done(copies):
    for c in copies:
        c.wait()


def forward(x, bufs):
    return dot(x, bufs[0][...]), dot(x, bufs[1][...]), dot_t(x, bufs[2][...])


def backward(h, bufs, width):
    return (
        dot_t(h[:, :width], bufs[0][...])
        + dot_t(h[:, width : 2 * width], bufs[1][...])
        + dot(h[:, 2 * width :], bufs[2][...])
    )


def call(kernel, outs, args, scratch, specs, flops, limit):
    moved = sum(a.size * a.dtype.itemsize for a, s in zip(args, specs) if s is VMEM)
    return pl.pallas_call(
        kernel,
        in_specs=specs,
        out_specs=[VMEM] * len(outs),
        out_shape=[jax.ShapeDtypeStruct(s, t) for s, t in outs],
        scratch_shapes=scratch,
        compiler_params=pltpu.CompilerParams(vmem_limit_bytes=limit * MIB),
        cost_estimate=pl.CostEstimate(flops=flops, bytes_accessed=moved + 4 * MIB, transcendentals=0),
    )(*args)


def partial_sums(plan, me, sources, sums, weights, limit):
    w = plan.width
    xs = [x for _, pieces in sources for x in pieces]
    rows = sum(x.shape[0] for x in sources[0][1])
    base = [] if sums is None else [sums]

    def kernel(me_ref, *refs):
        base_refs, x_refs = refs[: len(base)], list(refs[len(base) : len(base) + len(xs)])
        wg, wu, wd, out_ref = refs[len(base) + len(xs) : len(base) + len(xs) + 4]
        bufs, sems = refs[len(base) + len(xs) + 4 : -1], refs[-1]
        loads = [
            run(plan.copies(me_ref, k, DIRECT, plan.far, (wg, wu, wd), bufs[3 * i : 3 * i + 3], sems.at[i]))
            for i, (k, _) in enumerate(sources)
        ]
        for i, (_, pieces) in enumerate(sources):
            done(loads[i])
            first = 0
            for _ in pieces:
                x = x_refs.pop(0)
                last = first + x.shape[0]
                for t, term in enumerate(forward(x[...], bufs[3 * i : 3 * i + 3])):
                    cols = slice(t * w, (t + 1) * w)
                    if i > 0:
                        term = term + out_ref[first:last, cols]
                    elif base_refs:
                        term = term + base_refs[0][first:last, cols]
                    out_ref[first:last, cols] = term
                first = last

    return call(
        kernel,
        [((rows, 3 * w), F32)],
        (me, *base, *xs, *weights),
        plan.weight_scratch(plan.far) * len(sources) + [pltpu.SemaphoreType.DMA((len(sources), 3))],
        [SMEM] + [VMEM] * (len(base) + len(xs)) + [HBM] * 3,
        2 * rows * 3 * w * plan.far * len(sources),
        limit,
    )[0]


def gates(plan, me, sums, arrived, direct, weights):
    rows, w = sums.shape[0], plan.width
    half, block = rows // 2, 128
    order = (2,)
    n = len(order)
    near_cols = plan.parts * DIRECT

    def kernel(me_ref, sums_hbm, *refs):
        x_hbm, (direct_hbm, wg, wu, wd, out_ref, top_ref, bottom_ref, near_ref), rest = (
            refs[: 2 * n],
            refs[2 * n : 2 * n + 8],
            refs[2 * n + 8 :],
        )
        acc, x_buf, direct_buf = rest[:3]
        near, far, (n_sems, f_sems, x_sems, m_sems) = rest[3:6], rest[6:-4], rest[-4:]
        hbm = (wg, wu, wd)
        first_load = pltpu.make_async_copy(sums_hbm, acc, m_sems.at[0])
        first_load.start()
        loads = []
        for i, k in enumerate(order):
            weight_loads = run(plan.copies(me_ref, k, DIRECT, plan.far, hbm, far[3 * i : 3 * i + 3], f_sems.at[i]))
            x_loads = run(
                [pltpu.make_async_copy(x_hbm[2 * i + j], x_buf.at[2 * i + j], x_sems.at[2 * i + j]) for j in range(2)]
            )
            loads.append(weight_loads + x_loads)
        near_loads = [
            c
            for k in range(plan.parts)
            for c in run(plan.copies(me_ref, k, 0, DIRECT, hbm, near, n_sems.at[k], k * DIRECT))
        ]
        direct_load = pltpu.make_async_copy(direct_hbm, direct_buf, m_sems.at[1])
        direct_load.start()
        first_load.wait()
        for i in range(n):
            done(loads[i])
            for j in range(2):
                for t, term in enumerate(forward(x_buf[2 * i + j], far[3 * i : 3 * i + 3])):
                    acc[j * half : (j + 1) * half, t * w : (t + 1) * w] += term
        done(near_loads)
        direct_load.wait()
        for t, term in enumerate(forward(direct_buf[...], near)):
            acc[:, t * w : (t + 1) * w] += term

        @pl.loop(0, rows // block)
        def _(b):
            r = pl.ds(pl.multiple_of(b * block, block), block)
            gate, up = acc[r, 0:w], acc[r, w : 2 * w]
            back = pltpu.roll(acc[r, 2 * w : 3 * w], block - CAP, 0)
            first = lax.broadcasted_iota(jnp.int32, (block, w), 0) % (2 * CAP) < CAP
            sig = jax.nn.sigmoid(gate)
            act = gate * sig
            zero = jnp.zeros_like(act)
            grad_gate = back * up * sig * (1.0 + gate * (1.0 - sig))
            grad_up = back * act
            out_ref[r, 0:w] = jnp.where(first, zero, pltpu.roll(grad_gate, CAP, 0)).astype(BF16)
            out_ref[r, w : 2 * w] = jnp.where(first, zero, pltpu.roll(grad_up, CAP, 0)).astype(BF16)
            out_ref[r, 2 * w : 3 * w] = jnp.where(first, act * up, zero).astype(BF16)

        relay = backward(out_ref[...], far[-3:], w).astype(BF16)
        top_ref[...] = relay[:half]
        bottom_ref[...] = relay[half:]
        near_ref[...] = backward(out_ref[...], near, w).astype(BF16)

    scratch = [
        pltpu.VMEM((rows, 3 * w), F32),
        pltpu.VMEM((2 * n, half, plan.far), BF16),
        pltpu.VMEM((rows, near_cols), BF16),
        *plan.weight_scratch(near_cols),
        *(plan.weight_scratch(plan.far) * n),
        pltpu.SemaphoreType.DMA((plan.parts, 3)),
        pltpu.SemaphoreType.DMA((n, 3)),
        pltpu.SemaphoreType.DMA((2 * n,)),
        pltpu.SemaphoreType.DMA((2,)),
    ]
    return call(
        kernel,
        [
            ((rows, 3 * w), BF16),
            ((half, plan.far), BF16),
            ((half, plan.far), BF16),
            ((rows, near_cols), BF16),
        ],
        (me, sums, *arrived, direct, *weights),
        scratch,
        [SMEM] + [ANY] * (2 * n + 2) + [HBM] * 3,
        2 * rows * 3 * w * ((n + 1) * plan.far + 2 * near_cols),
        26,
    )


def products(plan, me, h, wanted, weights):
    w = plan.width
    reach = plan.far
    adds = [a for *_, a in wanted if a is not None]
    outs = [((last - first, reach), BF16) for _, first, last, _ in wanted]

    def kernel(me_ref, h_ref, *refs):
        add_refs = list(refs[: len(adds)])
        wg, wu, wd = refs[len(adds) : len(adds) + 3]
        out_refs = refs[len(adds) + 3 : len(adds) + 3 + len(outs)]
        bufs, sems = refs[len(adds) + 3 + len(outs) : -1], refs[-1]
        loads = [
            run(plan.copies(me_ref, k, DIRECT, reach, (wg, wu, wd), bufs[3 * i : 3 * i + 3], sems.at[i]))
            for i, (k, *_) in enumerate(wanted)
        ]
        for i, (_, first, last, extra) in enumerate(wanted):
            done(loads[i])
            value = backward(h_ref[first:last, :], bufs[3 * i : 3 * i + 3], w)
            if extra is not None:
                value = value + add_refs.pop(0)[...].astype(F32)
            out_refs[i][...] = value.astype(BF16)

    return call(
        kernel,
        outs,
        (me, h, *adds, *weights),
        plan.weight_scratch(reach) * len(wanted) + [pltpu.SemaphoreType.DMA((len(wanted), 3))],
        [SMEM] + [VMEM] * (1 + len(adds)) + [HBM] * 3,
        sum(2 * (last - first) * 3 * w * reach for _, first, last, _ in wanted),
        16,
    )


def per_device(tokens, routes, combine, w_gate, w_up, w_down, cotangent):
    toks, _ = tokens.shape
    sources = lax.axis_size("expert")
    parts = lax.axis_size("hidden")
    group = 2 * CAP
    rows = sources * group
    half = rows // 2
    plan = Plan(parts, w_gate.shape[1], w_gate.shape[2])
    me = lax.axis_index("hidden").astype(jnp.int32).reshape(1)
    weights = tuple(pltpu.with_memory_space_constraint(w[0], pltpu.HBM) for w in (w_gate, w_up, w_down))

    def shift(v, k):
        return lax.ppermute(v, "hidden", [(i, (i + k) % parts) for i in range(parts)])

    def exchange(v):
        out = lax.all_to_all(
            v.reshape(sources, group, v.shape[1]), "expert", split_axis=0, concat_axis=0, tiled=True
        )
        return out.reshape(rows, v.shape[1])

    table = jnp.concatenate([tokens, cotangent], axis=0)
    direct = table[:, :DIRECT]
    direct_parts = [direct] + [shift(direct, parts - k) for k in range(1, parts)]

    row = lax.broadcasted_iota(jnp.int32, (toks, rows), 1)
    owner = row // group
    hit = routes[:, :, None] == owner[:, None, :]
    named = jnp.any(hit, axis=1)
    weight = jnp.sum(jnp.where(hit, combine[:, :, None], 0.0), axis=1)
    earlier = (
        lax.broadcasted_iota(jnp.int32, (toks, toks), 0)
        > lax.broadcasted_iota(jnp.int32, (toks, toks), 1)
    ).astype(BF16)
    rank = dot(earlier, named.astype(BF16))
    placed = named & (rank.astype(jnp.int32) == row % CAP)
    is_token = row % group < CAP
    choose = jnp.concatenate([placed & is_token, placed & ~is_token], axis=0)
    select = choose.astype(BF16)

    def pack(values):
        return lax.dot_general(
            select, values, (((0,), (0,)), ((), ())), preferred_element_type=F32
        ).astype(BF16)

    own = exchange(pack(table[:, DIRECT:]))
    packed_direct = pack(jnp.concatenate(direct_parts, axis=1))
    own, packed_direct = lax.optimization_barrier((own, packed_direct))
    top, bottom = own[:half], own[half:]
    l_top = shift(top, 1)
    r_bottom = shift(bottom, -1)
    arrived_direct = exchange(packed_direct)
    l_bottom = shift(bottom, 1)
    r_top = shift(top, -1)
    o_top = shift(l_top, 1)
    o_bottom = shift(r_bottom, -1)
    sums = partial_sums(plan, me, [(0, [own])], None, weights, 14)
    sums = partial_sums(plan, me, [(3, [l_top, l_bottom]), (1, [r_top, r_bottom])], sums, weights, 18)
    grads, relay_top, relay_bottom, near = gates(plan, me, sums, (o_top, o_bottom), arrived_direct, weights)

    o_top = shift(relay_top, 1)
    o_bottom = shift(relay_bottom, -1)
    back_direct = exchange(near)
    p_bottom, p_top = products(plan, me, grads, [(1, half, rows, None), (3, 0, half, None)], weights)
    l_bottom = shift(p_bottom, 1)
    r_top = shift(p_top, -1)
    p_top, p_bottom = products(plan, me, grads, [(1, 0, half, o_top), (3, half, rows, o_bottom)], weights)
    l_top = shift(p_top, 1)
    r_bottom = shift(p_bottom, -1)
    mine = products(plan, me, grads, [(0, 0, rows, None)], weights)[0]
    total = (
        mine.astype(F32)
        + jnp.concatenate([l_top, l_bottom], axis=0).astype(F32)
        + jnp.concatenate([r_top, r_bottom], axis=0).astype(F32)
    ).astype(BF16)
    total, back_direct = lax.optimization_barrier((total, back_direct))
    back_far = exchange(total)

    spread = choose * jnp.concatenate([weight, weight], axis=0)
    coarse = lax.reduce_precision(spread, 8, 7)
    fine = (spread - coarse).astype(BF16)
    coarse = coarse.astype(BF16)

    def mix(back):
        return dot(coarse, back) + dot(fine, back)

    mixed = mix(back_direct)
    near = mixed[:, :DIRECT]
    for k in range(1, parts):
        near = near + shift(mixed[:, k * DIRECT : (k + 1) * DIRECT].astype(BF16), k).astype(F32)
    result = jnp.concatenate([near.astype(BF16), mix(back_far).astype(BF16)], axis=1)
    return result[:toks], result[toks:]


def solution(mesh):
    return jax.shard_map(
        per_device,
        mesh=mesh,
        in_specs=(
            P("expert", "hidden"),
            P("expert", None),
            P("expert", None),
            P("expert", None, "hidden"),
            P("expert", None, "hidden"),
            P("expert", "hidden", None),
            P("expert", "hidden"),
        ),
        out_specs=(P("expert", "hidden"), P("expert", "hidden")),
        check_vma=False,
    )
```

time: 265 us -> 239 us (0.902)
  matrix products: 27.3 us -> 7.91 us
  Pallas kernels: 9.92 us -> 26.9 us
  local copies, waits for them, and re-layouts: 19.9 us -> 7.73 us
  other arithmetic: 10.9 us -> 2.66 us
  waiting for transfers between devices: 127 us -> 123 us
    dot_general x18 -> x5, matrix products: 23 us -> 4.41 us  [dot(): return jnp.dot(a, b, preferred_element_type=F32)]
    pallas_call x1 -> x6, Pallas kernels: 9.92 us -> 26.9 us  [call(): pl.pallas_call(kernel, in_specs=specs, out_specs=[VMEM] * len(outs), out_...]
    ppermute x18, waiting for transfers between devices: 85.8 us -> 69.5 us  [shift(): lax.ppermute(v, 'hidden', [(i, (i + k) % parts) for i in range(parts)])]
    all_to_all x4, waiting for transfers between devices: 41.1 us -> 53.9 us  [exchange(): lax.all_to_all(v.reshape(sources, group, v.shape[1]), 'expert', split_axi...]
    dynamic_slice x12 -> x0, local copies, waits for them, and re-layouts: 12.2 us -> none  [the longest x10 8.32 us: relative(): lax.dynamic_slice_in_dim(w_down, start, hi - lo, 1)]
    concatenate x10 -> x1, other arithmetic: 10.2 us -> 0.67 us  [per_device(): jnp.concatenate([near.astype(BF16), mix(back_far).astype(BF16)], axis=1)]
    unnamed x49 -> x15, local copies, waits for them, and re-layouts: 4.02 us -> 5.69 us
  transfers between devices with their start and end apart: 22 -> 22, of which waited for: 12 -> 13; matrix products, arithmetic and copies ran while one was open for 16% -> 4% of each run, Pallas kernels for 0% -> 8%
where the time goes in v1:
time: 239 us; the launch traced here: 238 us
  waiting for transfers between devices  123 us (51%)
  starting transfers between devices  68.7 us (29%)
  Pallas kernels  26.9 us (11%)
  matrix products  7.91 us (3%)
  local copies, waits for them, and re-layouts  7.73 us (3%)
  other arithmetic  2.66 us (1%)
    ppermute x18, waiting for transfers between devices, shift(): lax.ppermute(v, 'hidden', [(i, (i + k) % parts) for i in range(parts)])  69.5 us
    all_to_all x4, waiting for transfers between devices, exchange(): lax.all_to_all(v.reshape(sources, group, v.shape[1]), 'expert', split_axi...  53.9 us
    all_to_all x4, starting transfers between devices, exchange(): lax.all_to_all(v.reshape(sources, group, v.shape[1]), 'expert', split_axi...  42.6 us
    pallas_call x6, Pallas kernels, call(): pl.pallas_call(kernel, in_specs=specs, out_specs=[VMEM] * len(outs), out_...  26.9 us
    ppermute x18, starting transfers between devices, shift(): lax.ppermute(v, 'hidden', [(i, (i + k) % parts) for i in range(parts)])  26.1 us
    unnamed x15, local copies, waits for them, and re-layouts  5.69 us
  transfers between devices with their start and end apart: 22, of which 13 were waited for; matrix products, arithmetic and copies ran while one was open for 4% of the time, Pallas kernels for 8%

profile of v1, /device:TPU:1, one launch (start us, length us, event | category | flops | bytes accessed | tf_op | source)
XLA Modules:
  0.0 238.2 jit_solution(17602300025600665171)
XLA Ops:
  5.1 13.0 %all-to-all-start = ((bf16[64,8,1408]{2,1,0:T(8,128)(2,1)}), bf16[64,8,1408]{2,1,0:T(8,128)(2,1)S(1)}, u32[]{:S(2)}, u32[]{:S(2)}) async-start(bf16[64,8,1408]{2,1,0:T(8,128)(2,1)} %fusion), calls=%async_computation | async-start | bytes 2883584 | tf_op jit(solution)/shard_map/all_to_all | solution.py:262
  26.9 28.2 %all-to-all-done = bf16[64,8,1408]{2,1,0:T(8,128)(2,1)S(1)} async-done(((bf16[64,8,1408]{2,1,0:T(8,128)(2,1)}), bf16[64,8,1408]{2,1,0:T(8,128)(2,1)S(1)}, u32[]{:S(2)}, u32[]{:S(2)}) %all-to-all-start) | async-done | bytes 1441824 | tf_op jit(solution)/shard_map/all_to_all | solution.py:262
  55.0 6.3 %all-to-all-start.1 = ((bf16[64,8,1536]{2,1,0:T(8,128)(2,1)}), bf16[64,8,1536]{2,1,0:T(8,128)(2,1)}, u32[]{:S(2)}, u32[]{:S(2)}) async-start(bf16[64,8,1536]{2,1,0:T(8,128)(2,1)} %bitcast.6), calls=%async_computation.1 | async-start | bytes 3145728 | tf_op jit(solution)/shard_map/all_to_all | solution.py:262
  62.5 2.7 %collective-permute-start.6 = (bf16[256,1408]{1,0:T(8,128)(2,1)}, bf16[256,1408]{1,0:T(8,128)(2,1)S(1)}, u32[]{:S(2)}, u32[]{:S(2)}) collective-permute-start(bf16[256,1408]{1,0:T(8,128)(2,1)} %get-tuple-element.26), channel_id=1, source_target_pairs={{0,3},{1,0},{2,1},{3,2},{4,7},{5,4},{6,5},{7,6},{8,11},{9,8},{10,9... | collective-permute-start | bytes 2162696 | tf_op jit(solution)/shard_map/ppermute | solution.py:259
  65.3 2.7 %collective-permute-start.5 = (bf16[256,1408]{1,0:T(8,128)(2,1)}, bf16[256,1408]{1,0:T(8,128)(2,1)}, u32[]{:S(2)}, u32[]{:S(2)}) collective-permute-start(bf16[256,1408]{1,0:T(8,128)(2,1)} %get-tuple-element.27), channel_id=1, source_target_pairs={{0,3},{1,0},{2,1},{3,2},{4,7},{5,4},{6,5},{7,6},{8,11},{9,8},{10,9... | collective-permute-start | bytes 2162696 | tf_op jit(solution)/shard_map/ppermute | solution.py:259
  68.0 12.6 %collective-permute-done.6.refs_4_ = bf16[256,1408]{1,0:T(8,128)(2,1)S(1)} collective-permute-done((bf16[256,1408]{1,0:T(8,128)(2,1)}, bf16[256,1408]{1,0:T(8,128)(2,1)S(1)}, u32[]{:S(2)}, u32[]{:S(2)}) %collective-permute-start.6) | collective-permute-done | bytes 720928 | tf_op jit(solution)/shard_map/ppermute | solution.py:259
  80.6 3.4 %collective-permute-start.8 = (bf16[256,1408]{1,0:T(8,128)(2,1)S(1)}, bf16[256,1408]{1,0:T(8,128)(2,1)}, u32[]{:S(2)}, u32[]{:S(2)}) collective-permute-start(bf16[256,1408]{1,0:T(8,128)(2,1)S(1)} %collective-permute-done.6.refs_4_), channel_id=1, source_target_pairs={{0,3},{1,0},{2,1},{3,2},{4,7},{5,4},{6,5},{7,6},{8,11},{9,8},{10,9... | collective-permute-start | bytes 2162696 | tf_op jit(solution)/shard_map/ppermute | solution.py:259
  84.0 3.0 %shard_map.86.refs_0_ = f32[512,768]{1,0:T(8,128)S(1)} custom-call(s32[1]{0:T(128)} %bitcast.me_ref, bf16[512,1408]{1,0:T(8,128)(2,1)S(1)} %bitcast.21, bf16[7168,256]{1,0:T(8,128)(2,1)} %bitcast.23, bf16[7168,256]{1,0:T(8,128)(2,1)} %bitcast.29, bf16[256,7168]{1,0:T(8,128)(2,1)} %bitcast.35), custom_call_target="tpu_custom_call" | custom-call | flops 1107296256 | bytes 5636096 | tf_op jit(solution)/shard_map/pallas_call | solution.py:73
  86.9 12.2 %collective-permute-done.4.refs_2_ = bf16[256,1408]{1,0:T(8,128)(2,1)S(1)} collective-permute-done((bf16[256,1408]{1,0:T(8,128)(2,1)}, bf16[256,1408]{1,0:T(8,128)(2,1)S(1)}, u32[]{:S(2)}, u32[]{:S(2)}) %collective-permute-start.4) | collective-permute-done | bytes 720928 | tf_op jit(solution)/shard_map/ppermute | solution.py:259
  101.1 5.7 %shard_map.87.sums_hbm = f32[512,768]{1,0:T(8,128)S(1)} custom-call(s32[1]{0:T(128)} %bitcast.me_ref, f32[512,768]{1,0:T(8,128)S(1)} %shard_map.86.refs_0_, bf16[256,1408]{1,0:T(8,128)(2,1)} %collective-permute-done.3.refs_1_, bf16[256,1408]{1,0:T(8,128)(2,1)S(1)} %copy-done.2, bf16[256,1408]{1,0:T(8,128)(2,1)} %collective-permute-done.5.refs_3_, ...), custom_call_target="tpu_custom_call" | custom-call | flops 2214592512 | bytes 8650752 | tf_op jit(solution)/shard_map/pallas_call | solution.py:73
  106.8 4.6 %collective-permute-done.8.refs_1_ = bf16[256,1408]{1,0:T(8,128)(2,1)} collective-permute-done((bf16[256,1408]{1,0:T(8,128)(2,1)S(1)}, bf16[256,1408]{1,0:T(8,128)(2,1)}, u32[]{:S(2)}, u32[]{:S(2)}) %collective-permute-start.8) | collective-permute-done | bytes 720928 | tf_op jit(solution)/shard_map/ppermute | solution.py:259
  111.4 3.2 %collective-permute-done.7.refs_0_ = bf16[256,1408]{1,0:T(8,128)(2,1)} collective-permute-done((bf16[256,1408]{1,0:T(8,128)(2,1)}, bf16[256,1408]{1,0:T(8,128)(2,1)}, u32[]{:S(2)}, u32[]{:S(2)}) %collective-permute-start.7) | collective-permute-done | bytes 720928 | tf_op jit(solution)/shard_map/ppermute | solution.py:259
  114.6 8.8 %shard_map.88 = (bf16[512,768]{1,0:T(8,128)(2,1)S(1)}, bf16[256,1408]{1,0:T(8,128)(2,1)S(1)}, bf16[256,1408]{1,0:T(8,128)(2,1)S(1)}, bf16[512,1536]{1,0:T(8,128)(2,1)S(1)}) custom-call(s32[1]{0:T(128)} %bitcast.me_ref, f32[512,768]{1,0:T(8,128)S(1)} %shard_map.87.sums_hbm, bf16[256,1408]{1,0:T(8,128)(2,1)} %collective-permute-done.7.refs_0_, ...), custom_call_target="tpu_custom_call" | custom-call | flops 4630511616 | bytes 4194304 | tf_op jit(solution)/shard_map/pallas_call | solution.py:73
  125.5 11.9 %all-to-all-start.2 = ((bf16[64,8,1536]{2,1,0:T(8,128)(2,1)}), bf16[64,8,1536]{2,1,0:T(8,128)(2,1)}, u32[]{:S(2)}, u32[]{:S(2)}) async-start(bf16[64,8,1536]{2,1,0:T(8,128)(2,1)} %bitcast.22), calls=%async_computation.2 | async-start | bytes 3145728 | tf_op jit(solution)/shard_map/all_to_all | solution.py:262
  140.1 3.2 %shard_map.91 = (bf16[256,1408]{1,0:T(8,128)(2,1)S(1)}, bf16[256,1408]{1,0:T(8,128)(2,1)S(1)}) custom-call(s32[1]{0:T(128)} %bitcast.me_ref, bf16[512,768]{1,0:T(8,128)(2,1)S(1)} %get-tuple-element.16.h_ref, bf16[7168,256]{1,0:T(8,128)(2,1)} %bitcast.26, bf16[7168,256]{1,0:T(8,128)(2,1)} %bitcast.32, bf16[256,7168]{1,0:T(8,128)(2,1)} %bitcast.38), custom_call_target="tpu_custom_call" | custom-call | flops 1107296256 | bytes 4980736 | tf_op jit(solution)/shard_map/pallas_call | solution.py:73
  146.1 9.8 %collective-permute-done.9.refs_0_ = bf16[256,1408]{1,0:T(8,128)(2,1)S(1)} collective-permute-done((bf16[256,1408]{1,0:T(8,128)(2,1)S(1)}, bf16[256,1408]{1,0:T(8,128)(2,1)S(1)}, u32[]{:S(2)}, u32[]{:S(2)}) %collective-permute-start.9) | collective-permute-done | bytes 720928 | tf_op jit(solution)/shard_map/ppermute | solution.py:259
  155.9 3.2 %shard_map.90 = (bf16[256,1408]{1,0:T(8,128)(2,1)S(1)}, bf16[256,1408]{1,0:T(8,128)(2,1)S(1)}) custom-call(s32[1]{0:T(128)} %bitcast.me_ref, bf16[512,768]{1,0:T(8,128)(2,1)S(1)} %get-tuple-element.16.h_ref, bf16[256,1408]{1,0:T(8,128)(2,1)S(1)} %collective-permute-done.9.refs_0_, bf16[256,1408]{1,0:T(8,128)(2,1)S(1)} %collective-permute-done.10.refs_1_, ...), custom_call_target="tpu_custom_call" | custom-call | flops 1107296256 | bytes 6422528 | tf_op jit(solution)/shard_map/pallas_call | solution.py:73
  161.9 3.0 %shard_map.89 = bf16[512,1408]{1,0:T(8,128)(2,1)S(1)} custom-call(s32[1]{0:T(128)} %bitcast.me_ref, bf16[512,768]{1,0:T(8,128)(2,1)S(1)} %get-tuple-element.16.h_ref, bf16[7168,256]{1,0:T(8,128)(2,1)} %bitcast.28, bf16[7168,256]{1,0:T(8,128)(2,1)} %bitcast.34, bf16[256,7168]{1,0:T(8,128)(2,1)} %bitcast.40), custom_call_target="tpu_custom_call" | custom-call | flops 1107296256 | bytes 4980736 | tf_op jit(solution)/shard_map/pallas_call | solution.py:73
  164.9 6.5 %collective-permute-done.12 = bf16[256,1408]{1,0:T(8,128)(2,1)S(1)} collective-permute-done((bf16[256,1408]{1,0:T(8,128)(2,1)S(1)}, bf16[256,1408]{1,0:T(8,128)(2,1)S(1)}, u32[]{:S(2)}, u32[]{:S(2)}) %collective-permute-start.12) | collective-permute-done | bytes 720928 | tf_op jit(solution)/shard_map/ppermute | solution.py:259
  171.4 15.3 %collective-permute-done.11 = bf16[256,1408]{1,0:T(8,128)(2,1)S(1)} collective-permute-done((bf16[256,1408]{1,0:T(8,128)(2,1)S(1)}, bf16[256,1408]{1,0:T(8,128)(2,1)S(1)}, u32[]{:S(2)}, u32[]{:S(2)}) %collective-permute-start.11) | collective-permute-done | bytes 720928 | tf_op jit(solution)/shard_map/ppermute | solution.py:259
  188.4 11.4 %all-to-all-start.3 = ((bf16[64,8,1408]{2,1,0:T(8,128)(2,1)}), bf16[64,8,1408]{2,1,0:T(8,128)(2,1)S(1)}, u32[]{:S(2)}, u32[]{:S(2)}) async-start(bf16[64,8,1408]{2,1,0:T(8,128)(2,1)} %bitcast.10), calls=%async_computation.3 | async-start | bytes 2883584 | tf_op jit(solution)/shard_map/all_to_all | solution.py:262
  203.8 2.7 %collective-permute-start.17 = (bf16[32,384]{1,0:T(8,128)(2,1)S(1)}, bf16[32,384]{1,0:T(8,128)(2,1)S(1)}, u32[]{:S(2)}, u32[]{:S(2)}) collective-permute-start(bf16[32,384]{1,0:T(8,128)(2,1)S(1)} %get-tuple-element.31), channel_id=1, source_target_pairs={{0,3},{1,0},{2,1},{3,2},{4,7},{5,4},{6,5},{7,6},{8,11},{9,8},{10,9... | collective-permute-start | bytes 73736 | tf_op jit(solution)/shard_map/ppermute | solution.py:259
  207.9 3.0 %collective-permute-done.16 = bf16[32,384]{1,0:T(8,128)(2,1)S(1)} collective-permute-done((bf16[32,384]{1,0:T(8,128)(2,1)S(1)}, bf16[32,384]{1,0:T(8,128)(2,1)S(1)}, u32[]{:S(2)}, u32[]{:S(2)}) %collective-permute-start.16) | collective-permute-done | bytes 24608 | tf_op jit(solution)/shard_map/ppermute | solution.py:259
  211.0 25.8 %all-to-all-done.3 = bf16[64,8,1408]{2,1,0:T(8,128)(2,1)S(1)} async-done(((bf16[64,8,1408]{2,1,0:T(8,128)(2,1)}), bf16[64,8,1408]{2,1,0:T(8,128)(2,1)S(1)}, u32[]{:S(2)}, u32[]{:S(2)}) %all-to-all-start.3) | async-done | bytes 1441824 | tf_op jit(solution)/shard_map/all_to_all | solution.py:262
  (63 shorter events, 35.1 us)
Async XLA Ops:
  5.1 49.9 %all-to-all-start = ((bf16[64,8,1408]{2,1,0:T(8,128)(2,1)}), bf16[64,8,1408]{2,1,0:T(8,128)(2,1)S(1)}, u32[]{:S(2)}, u32[]{:S(2)}) async-start(bf16[64,8,1408]{2,1,0:T(8,128)(2,1)} %fusion), calls=%async_computation | async-start | bytes 2883584 | tf_op jit(solution)/shard_map/all_to_all | solution.py:262
  18.1 5.1 %collective-permute-start.2 = (bf16[32,384]{1,0:T(8,128)(2,1)S(1)}, bf16[32,384]{1,0:T(8,128)(2,1)S(1)}, u32[]{:S(2)}, u32[]{:S(2)}) collective-permute-start(bf16[32,384]{1,0:T(8,128)(2,1)S(1)} %slice.44), channel_id=1, source_target_pairs={{0,1},{1,2},{2,3},{3,0},{4,5},{5,6},{6,7},{7,4},{8,9},{9,10},{10,1... | collective-permute-start | bytes 73736 | tf_op jit(solution)/shard_map/ppermute | solution.py:259
  19.5 4.3 %collective-permute-start.1 = (bf16[32,384]{1,0:T(8,128)(2,1)S(1)}, bf16[32,384]{1,0:T(8,128)(2,1)S(1)}, u32[]{:S(2)}, u32[]{:S(2)}) collective-permute-start(bf16[32,384]{1,0:T(8,128)(2,1)S(1)} %slice.44), channel_id=1, source_target_pairs={{0,2},{1,3},{2,0},{3,1},{4,6},{5,7},{6,4},{7,5},{8,10},{9,11},{10,... | collective-permute-start | bytes 73736 | tf_op jit(solution)/shard_map/ppermute | solution.py:259
  22.1 3.0 %collective-permute-start = (bf16[32,384]{1,0:T(8,128)(2,1)S(1)}, bf16[32,384]{1,0:T(8,128)(2,1)S(1)}, u32[]{:S(2)}, u32[]{:S(2)}) collective-permute-start(bf16[32,384]{1,0:T(8,128)(2,1)S(1)} %slice.44), channel_id=1, source_target_pairs={{0,3},{1,0},{2,1},{3,2},{4,7},{5,4},{6,5},{7,6},{8,11},{9,8},{10,9... | collective-permute-start | bytes 73736 | tf_op jit(solution)/shard_map/ppermute | solution.py:259
  55.0 59.6 %all-to-all-start.1 = ((bf16[64,8,1536]{2,1,0:T(8,128)(2,1)}), bf16[64,8,1536]{2,1,0:T(8,128)(2,1)}, u32[]{:S(2)}, u32[]{:S(2)}) async-start(bf16[64,8,1536]{2,1,0:T(8,128)(2,1)} %bitcast.6), calls=%async_computation.1 | async-start | bytes 3145728 | tf_op jit(solution)/shard_map/all_to_all | solution.py:262
  62.5 18.0 %collective-permute-start.6 = (bf16[256,1408]{1,0:T(8,128)(2,1)}, bf16[256,1408]{1,0:T(8,128)(2,1)S(1)}, u32[]{:S(2)}, u32[]{:S(2)}) collective-permute-start(bf16[256,1408]{1,0:T(8,128)(2,1)} %get-tuple-element.26), channel_id=1, source_target_pairs={{0,3},{1,0},{2,1},{3,2},{4,7},{5,4},{6,5},{7,6},{8,11},{9,8},{10,9... | collective-permute-start | bytes 2162696 | tf_op jit(solution)/shard_map/ppermute | solution.py:259
  65.3 18.7 %collective-permute-start.3 = (bf16[256,1408]{1,0:T(8,128)(2,1)}, bf16[256,1408]{1,0:T(8,128)(2,1)}, u32[]{:S(2)}, u32[]{:S(2)}) collective-permute-start(bf16[256,1408]{1,0:T(8,128)(2,1)} %get-tuple-element.27), channel_id=1, source_target_pairs={{0,1},{1,2},{2,3},{3,0},{4,5},{5,6},{6,7},{7,4},{8,9},{9,10},{10,1... | collective-permute-start | bytes 2162696 | tf_op jit(solution)/shard_map/ppermute | solution.py:259
  65.3 33.9 %collective-permute-start.4 = (bf16[256,1408]{1,0:T(8,128)(2,1)}, bf16[256,1408]{1,0:T(8,128)(2,1)S(1)}, u32[]{:S(2)}, u32[]{:S(2)}) collective-permute-start(bf16[256,1408]{1,0:T(8,128)(2,1)} %get-tuple-element.26), channel_id=1, source_target_pairs={{0,1},{1,2},{2,3},{3,0},{4,5},{5,6},{6,7},{7,4},{8,9},{9,10},{10,1... | collective-permute-start | bytes 2162696 | tf_op jit(solution)/shard_map/ppermute | solution.py:259
  65.3 34.7 %collective-permute-start.5 = (bf16[256,1408]{1,0:T(8,128)(2,1)}, bf16[256,1408]{1,0:T(8,128)(2,1)}, u32[]{:S(2)}, u32[]{:S(2)}) collective-permute-start(bf16[256,1408]{1,0:T(8,128)(2,1)} %get-tuple-element.27), channel_id=1, source_target_pairs={{0,3},{1,0},{2,1},{3,2},{4,7},{5,4},{6,5},{7,6},{8,11},{9,8},{10,9... | collective-permute-start | bytes 2162696 | tf_op jit(solution)/shard_map/ppermute | solution.py:259
  80.6 30.8 %collective-permute-start.8 = (bf16[256,1408]{1,0:T(8,128)(2,1)S(1)}, bf16[256,1408]{1,0:T(8,128)(2,1)}, u32[]{:S(2)}, u32[]{:S(2)}) collective-permute-start(bf16[256,1408]{1,0:T(8,128)(2,1)S(1)} %collective-permute-done.6.refs_4_), channel_id=1, source_target_pairs={{0,3},{1,0},{2,1},{3,2},{4,7},{5,4},{6,5},{7,6},{8,11},{9,8},{10,9... | collective-permute-start | bytes 2162696 | tf_op jit(solution)/shard_map/ppermute | solution.py:259
  84.0 30.6 %collective-permute-start.7 = (bf16[256,1408]{1,0:T(8,128)(2,1)}, bf16[256,1408]{1,0:T(8,128)(2,1)}, u32[]{:S(2)}, u32[]{:S(2)}) collective-permute-start(bf16[256,1408]{1,0:T(8,128)(2,1)} %collective-permute-done.3.refs_1_), channel_id=1, source_target_pairs={{0,1},{1,2},{2,3},{3,0},{4,5},{5,6},{6,7},{7,4},{8,9},{9,10},{10,1... | collective-permute-start | bytes 2162696 | tf_op jit(solution)/shard_map/ppermute | solution.py:259
  125.5 11.9 %copy-start.4 = (bf16[256,1408]{1,0:T(8,128)(2,1)S(1)}, bf16[256,1408]{1,0:T(8,128)(2,1)}, u32[]{:S(2)}) copy-start(bf16[256,1408]{1,0:T(8,128)(2,1)} %copy-done.3) | copy-start | bytes 2162692
  125.5 62.9 %all-to-all-start.2 = ((bf16[64,8,1536]{2,1,0:T(8,128)(2,1)}), bf16[64,8,1536]{2,1,0:T(8,128)(2,1)}, u32[]{:S(2)}, u32[]{:S(2)}) async-start(bf16[64,8,1536]{2,1,0:T(8,128)(2,1)} %bitcast.22), calls=%async_computation.2 | async-start | bytes 3145728 | tf_op jit(solution)/shard_map/all_to_all | solution.py:262
  137.4 18.6 %collective-permute-start.9 = (bf16[256,1408]{1,0:T(8,128)(2,1)S(1)}, bf16[256,1408]{1,0:T(8,128)(2,1)S(1)}, u32[]{:S(2)}, u32[]{:S(2)}) collective-permute-start(bf16[256,1408]{1,0:T(8,128)(2,1)S(1)} %copy-done.4), channel_id=1, source_target_pairs={{0,1},{1,2},{2,3},{3,0},{4,5},{5,6},{6,7},{7,4},{8,9},{9,10},{10,1... | collective-permute-start | bytes 2162696 | tf_op jit(solution)/shard_map/ppermute | solution.py:259
  137.5 18.5 %collective-permute-start.10 = (bf16[256,1408]{1,0:T(8,128)(2,1)S(1)}, bf16[256,1408]{1,0:T(8,128)(2,1)S(1)}, u32[]{:S(2)}, u32[]{:S(2)}) collective-permute-start(bf16[256,1408]{1,0:T(8,128)(2,1)S(1)} %get-tuple-element.18), channel_id=1, source_target_pairs={{0,3},{1,0},{2,1},{3,2},{4,7},{5,4},{6,5},{7,6},{8,11},{9,8},{10,9... | collective-permute-start | bytes 2162696 | tf_op jit(solution)/shard_map/ppermute | solution.py:259
  143.4 28.0 %collective-permute-start.12 = (bf16[256,1408]{1,0:T(8,128)(2,1)S(1)}, bf16[256,1408]{1,0:T(8,128)(2,1)S(1)}, u32[]{:S(2)}, u32[]{:S(2)}) collective-permute-start(bf16[256,1408]{1,0:T(8,128)(2,1)S(1)} %get-tuple-element.20), channel_id=1, source_target_pairs={{0,1},{1,2},{2,3},{3,0},{4,5},{5,6},{6,7},{7,4},{8,9},{9,10},{10,1... | collective-permute-start | bytes 2162696 | tf_op jit(solution)/shard_map/ppermute | solution.py:259
  143.5 27.9 %collective-permute-start.13 = (bf16[256,1408]{1,0:T(8,128)(2,1)S(1)}, bf16[256,1408]{1,0:T(8,128)(2,1)S(1)}, u32[]{:S(2)}, u32[]{:S(2)}) collective-permute-start(bf16[256,1408]{1,0:T(8,128)(2,1)S(1)} %get-tuple-element.21), channel_id=1, source_target_pairs={{0,3},{1,0},{2,1},{3,2},{4,7},{5,4},{6,5},{7,6},{8,11},{9,8},{10,9... | collective-permute-start | bytes 2162696 | tf_op jit(solution)/shard_map/ppermute | solution.py:259
  159.2 27.6 %collective-permute-start.11 = (bf16[256,1408]{1,0:T(8,128)(2,1)S(1)}, bf16[256,1408]{1,0:T(8,128)(2,1)S(1)}, u32[]{:S(2)}, u32[]{:S(2)}) collective-permute-start(bf16[256,1408]{1,0:T(8,128)(2,1)S(1)} %get-tuple-element.19), channel_id=1, source_target_pairs={{0,1},{1,2},{2,3},{3,0},{4,5},{5,6},{6,7},{7,4},{8,9},{9,10},{10,1... | collective-permute-start | bytes 2162696 | tf_op jit(solution)/shard_map/ppermute | solution.py:259
  159.3 27.5 %collective-permute-start.14 = (bf16[256,1408]{1,0:T(8,128)(2,1)S(1)}, bf16[256,1408]{1,0:T(8,128)(2,1)S(1)}, u32[]{:S(2)}, u32[]{:S(2)}) collective-permute-start(bf16[256,1408]{1,0:T(8,128)(2,1)S(1)} %get-tuple-element.22), channel_id=1, source_target_pairs={{0,3},{1,0},{2,1},{3,2},{4,7},{5,4},{6,5},{7,6},{8,11},{9,8},{10,9... | collective-permute-start | bytes 2162696 | tf_op jit(solution)/shard_map/ppermute | solution.py:259
  188.4 11.5 %copy-start.5 = (f32[16,8]{0,1:T(8,128)S(1)}, f32[16,8]{0,1:T(8,128)}, u32[]{:S(2)}) copy-start(f32[16,8]{0,1:T(8,128)} %param.9) | copy-start | bytes 1540
  188.4 48.4 %all-to-all-start.3 = ((bf16[64,8,1408]{2,1,0:T(8,128)(2,1)}), bf16[64,8,1408]{2,1,0:T(8,128)(2,1)S(1)}, u32[]{:S(2)}, u32[]{:S(2)}) async-start(bf16[64,8,1408]{2,1,0:T(8,128)(2,1)} %bitcast.10), calls=%async_computation.3 | async-start | bytes 2883584 | tf_op jit(solution)/shard_map/all_to_all | solution.py:262
  203.7 4.3 %collective-permute-start.15 = (bf16[32,384]{1,0:T(8,128)(2,1)S(1)}, bf16[32,384]{1,0:T(8,128)(2,1)S(1)}, u32[]{:S(2)}, u32[]{:S(2)}) collective-permute-start(bf16[32,384]{1,0:T(8,128)(2,1)S(1)} %get-tuple-element.30), channel_id=1, source_target_pairs={{0,1},{1,2},{2,3},{3,0},{4,5},{5,6},{6,7},{7,4},{8,9},{9,10},{10,1... | collective-permute-start | bytes 73736 | tf_op jit(solution)/shard_map/ppermute | solution.py:259
  203.8 4.2 %collective-permute-start.17 = (bf16[32,384]{1,0:T(8,128)(2,1)S(1)}, bf16[32,384]{1,0:T(8,128)(2,1)S(1)}, u32[]{:S(2)}, u32[]{:S(2)}) collective-permute-start(bf16[32,384]{1,0:T(8,128)(2,1)S(1)} %get-tuple-element.31), channel_id=1, source_target_pairs={{0,3},{1,0},{2,1},{3,2},{4,7},{5,4},{6,5},{7,6},{8,11},{9,8},{10,9... | collective-permute-start | bytes 73736 | tf_op jit(solution)/shard_map/ppermute | solution.py:259
  206.5 4.5 %collective-permute-start.16 = (bf16[32,384]{1,0:T(8,128)(2,1)S(1)}, bf16[32,384]{1,0:T(8,128)(2,1)S(1)}, u32[]{:S(2)}, u32[]{:S(2)}) collective-permute-start(bf16[32,384]{1,0:T(8,128)(2,1)S(1)} %get-tuple-element.32), channel_id=1, source_target_pairs={{0,2},{1,3},{2,0},{3,1},{4,6},{5,7},{6,4},{7,5},{8,10},{9,11},{10,... | collective-permute-start | bytes 73736 | tf_op jit(solution)/shard_map/ppermute | solution.py:259
  (4 other events, 4.0 us)

commit v2 on v1

--- a/solution.py
+++ b/solution.py
@@ -68,17 +68,85 @@
     )
 
 
-def call(kernel, outs, args, scratch, specs, flops, limit):
+def call(kernel, outs, args, scratch, specs, flops, limit, out_specs=None):
     moved = sum(a.size * a.dtype.itemsize for a, s in zip(args, specs) if s is VMEM)
     return pl.pallas_call(
         kernel,
         in_specs=specs,
-        out_specs=[VMEM] * len(outs),
-        out_shape=[jax.ShapeDtypeStruct(s, t) for s, t in outs],
+        out_specs=out_specs or [VMEM] * len(outs),
+        out_shape=[
+            pltpu.HBM(s, t) if spec is HBM else jax.ShapeDtypeStruct(s, t)
+            for (s, t), spec in zip(outs, out_specs or [VMEM] * len(outs))
+        ],
         scratch_shapes=scratch,
         compiler_params=pltpu.CompilerParams(vmem_limit_bytes=limit * MIB),
         cost_estimate=pl.CostEstimate(flops=flops, bytes_accessed=moved + 4 * MIB, transcendentals=0),
     )(*args)
+
+
+def pack_far(tokens, routes, cotangent, rows):
+    toks, picks = routes.shape
+    group = 2 * CAP
+    experts = rows // group
+    far = tokens.shape[1] - DIRECT
+
+    def kernel(tok_hbm, routes_hbm, cot_hbm, out_ref, select_ref, table_ref, routes_ref, sems):
+        loads = run(
+            [
+                pltpu.make_async_copy(routes_hbm, routes_ref, sems.at[0]),
+                pltpu.make_async_copy(tok_hbm, table_ref.at[:toks], sems.at[1]),
+                pltpu.make_async_copy(cot_hbm, table_ref.at[toks:], sems.at[2]),
+            ]
+        )
+        row = lax.broadcasted_iota(jnp.int32, (toks, rows), 1)
+        expert = lax.broadcasted_iota(jnp.int32, (experts, toks), 0)
+        loads[0].wait()
+        wanted = routes_ref[0:1, :] == expert
+        for k in range(1, picks):
+            wanted = wanted | (routes_ref[k : k + 1, :] == expert)
+        spread = lax.broadcasted_iota(jnp.int32, (experts, rows), 1) // group == lax.broadcasted_iota(
+            jnp.int32, (experts, rows), 0
+        )
+        named = (
+            lax.dot_general(
+                wanted.astype(F32).astype(BF16),
+                spread.astype(F32).astype(BF16),
+                (((0,), (0,)), ((), ())),
+                preferred_element_type=F32,
+            )
+            > 0.5
+        )
+        earlier = (
+            lax.broadcasted_iota(jnp.int32, (toks, toks), 0)
+            > lax.broadcasted_iota(jnp.int32, (toks, toks), 1)
+        ).astype(BF16)
+        rank = dot(earlier, named.astype(F32).astype(BF16)).astype(jnp.int32)
+        placed = named & (rank == row % CAP)
+        is_token = row % group < CAP
+        one, none = jnp.ones((toks, rows), F32), jnp.zeros((toks, rows), F32)
+        select = jnp.concatenate(
+            [jnp.where(placed & is_token, one, none), jnp.where(placed & ~is_token, one, none)], axis=0
+        ).astype(BF16)
+        select_ref[...] = select
+        done(loads[1:])
+        table = table_ref[:, DIRECT:]
+        out_ref[...] = lax.dot_general(
+            select, table, (((0,), (0,)), ((), ())), preferred_element_type=F32
+        ).astype(BF16)
+
+    return call(
+        kernel,
+        [((rows, far), BF16), ((2 * toks, rows), BF16)],
+        [pltpu.with_memory_space_constraint(v, pltpu.HBM) for v in (tokens, routes.T, cotangent)],
+        [
+            pltpu.VMEM((2 * toks, tokens.shape[1]), BF16),
+            pltpu.VMEM((picks, toks), jnp.int32),
+            pltpu.SemaphoreType.DMA((3,)),
+        ],
+        [HBM] * 3,
+        4 * toks * rows * far,
+        12,
+    )
 
 
 def partial_sums(plan, me, sources, sums, weights, limit):
@@ -121,7 +189,7 @@
     )[0]
 
 
-def gates(plan, me, sums, arrived, direct, weights):
+def gates(plan, me, sums, arrived, weights):
     rows, w = sums.shape[0], plan.width
     half, block = rows // 2, 128
     order = (2,)
@@ -129,10 +197,10 @@
     near_cols = plan.parts * DIRECT
 
     def kernel(me_ref, sums_hbm, *refs):
-        x_hbm, (direct_hbm, wg, wu, wd, out_ref, top_ref, bottom_ref, near_ref), rest = (
+        x_hbm, (wg, wu, wd, out_ref, top_ref, bottom_ref, near_ref), rest = (
             refs[: 2 * n],
-            refs[2 * n : 2 * n + 8],
-            refs[2 * n + 8 :],
+            refs[2 * n : 2 * n + 7],
+            refs[2 * n + 7 :],
         )
         acc, x_buf, direct_buf = rest[:3]
         near, far, (n_sems, f_sems, x_sems, m_sems) = rest[3:6], rest[6:-4], rest[-4:]
@@ -151,18 +219,12 @@
             for k in range(plan.parts)
             for c in run(plan.copies(me_ref, k, 0, DIRECT, hbm, near, n_sems.at[k], k * DIRECT))
         ]
-        direct_load = pltpu.make_async_copy(direct_hbm, direct_buf, m_sems.at[1])
-        direct_load.start()
         first_load.wait()
         for i in range(n):
             done(loads[i])
             for j in range(2):
                 for t, term in enumerate(forward(x_buf[2 * i + j], far[3 * i : 3 * i + 3])):
                     acc[j * half : (j + 1) * half, t * w : (t + 1) * w] += term
-        done(near_loads)
-        direct_load.wait()
-        for t, term in enumerate(forward(direct_buf[...], near)):
-            acc[:, t * w : (t + 1) * w] += term
 
         @pl.loop(0, rows // block)
         def _(b):
@@ -179,10 +241,14 @@
             out_ref[r, w : 2 * w] = jnp.where(first, zero, pltpu.roll(grad_up, CAP, 0)).astype(BF16)
             out_ref[r, 2 * w : 3 * w] = jnp.where(first, act * up, zero).astype(BF16)
 
+        done(near_loads)
+        direct_buf[...] = backward(out_ref[...], near, w).astype(BF16)
+        store = pltpu.make_async_copy(direct_buf, near_ref, m_sems.at[2])
+        store.start()
         relay = backward(out_ref[...], far[-3:], w).astype(BF16)
         top_ref[...] = relay[:half]
         bottom_ref[...] = relay[half:]
-        near_ref[...] = backward(out_ref[...], near, w).astype(BF16)
+        store.wait()
 
     scratch = [
         pltpu.VMEM((rows, 3 * w), F32),
@@ -193,9 +259,9 @@
         pltpu.SemaphoreType.DMA((plan.parts, 3)),
         pltpu.SemaphoreType.DMA((n, 3)),
         pltpu.SemaphoreType.DMA((2 * n,)),
-        pltpu.SemaphoreType.DMA((2,)),
+        pltpu.SemaphoreType.DMA((3,)),
     ]
-    return call(
+    out = call(
         kernel,
         [
             ((rows, 3 * w), BF16),
@@ -203,12 +269,38 @@
             ((half, plan.far), BF16),
             ((rows, near_cols), BF16),
         ],
-        (me, sums, *arrived, direct, *weights),
+        (me, sums, *arrived, *weights),
         scratch,
-        [SMEM] + [ANY] * (2 * n + 2) + [HBM] * 3,
-        2 * rows * 3 * w * ((n + 1) * plan.far + 2 * near_cols),
+        [SMEM] + [ANY] * (2 * n + 1) + [HBM] * 3,
+        2 * rows * 3 * w * ((n + 1) * plan.far + near_cols),
         26,
-    )
+        [VMEM, VMEM, VMEM, HBM],
+    )
+    return out
+
+
+def near_sums(plan, me, sums, direct, weights):
+    rows, w = sums.shape[0], plan.width
+    near_cols = plan.parts * DIRECT
+
+    def kernel(me_ref, sums_ref, x_ref, wg, wu, wd, out_ref, g, u, d, sems):
+        loads = []
+        for k in range(plan.parts):
+            loads += run(plan.copies(me_ref, k, 0, DIRECT, (wg, wu, wd), (g, u, d), sems.at[k], k * DIRECT))
+        done(loads)
+        for t, term in enumerate(forward(x_ref[...], (g, u, d))):
+            c = slice(t * w, (t + 1) * w)
+            out_ref[:, c] = sums_ref[:, c] + term
+
+    return call(
+        kernel,
+        [((rows, 3 * w), F32)],
+        (me, sums, direct, *weights),
+        plan.weight_scratch(near_cols) + [pltpu.SemaphoreType.DMA((plan.parts, 3))],
+        [SMEM, VMEM, VMEM, HBM, HBM, HBM],
+        2 * rows * 3 * w * near_cols,
+        16,
+    )[0]
 
 
 def products(plan, me, h, wanted, weights):
@@ -253,7 +345,9 @@
     half = rows // 2
     plan = Plan(parts, w_gate.shape[1], w_gate.shape[2])
     me = lax.axis_index("hidden").astype(jnp.int32).reshape(1)
-    weights = tuple(pltpu.with_memory_space_constraint(w[0], pltpu.HBM) for w in (w_gate, w_up, w_down))
+    weights = tuple(
+        pltpu.with_memory_space_constraint(w[0], pltpu.HBM) for w in (w_gate, w_up, w_down)
+    )
 
     def shift(v, k):
         return lax.ppermute(v, "hidden", [(i, (i + k) % parts) for i in range(parts)])
@@ -264,31 +358,17 @@
         )
         return out.reshape(rows, v.shape[1])
 
-    table = jnp.concatenate([tokens, cotangent], axis=0)
-    direct = table[:, :DIRECT]
+    direct = jnp.concatenate([tokens[:, :DIRECT], cotangent[:, :DIRECT]], axis=0)
     direct_parts = [direct] + [shift(direct, parts - k) for k in range(1, parts)]
 
-    row = lax.broadcasted_iota(jnp.int32, (toks, rows), 1)
-    owner = row // group
-    hit = routes[:, :, None] == owner[:, None, :]
-    named = jnp.any(hit, axis=1)
-    weight = jnp.sum(jnp.where(hit, combine[:, :, None], 0.0), axis=1)
-    earlier = (
-        lax.broadcasted_iota(jnp.int32, (toks, toks), 0)
-        > lax.broadcasted_iota(jnp.int32, (toks, toks), 1)
-    ).astype(BF16)
-    rank = dot(earlier, named.astype(BF16))
-    placed = named & (rank.astype(jnp.int32) == row % CAP)
-    is_token = row % group < CAP
-    choose = jnp.concatenate([placed & is_token, placed & ~is_token], axis=0)
-    select = choose.astype(BF16)
+    packed_far, select = pack_far(tokens, routes, cotangent, rows)
 
     def pack(values):
         return lax.dot_general(
             select, values, (((0,), (0,)), ((), ())), preferred_element_type=F32
         ).astype(BF16)
 
-    own = exchange(pack(table[:, DIRECT:]))
+    own = exchange(packed_far)
     packed_direct = pack(jnp.concatenate(direct_parts, axis=1))
     own, packed_direct = lax.optimization_barrier((own, packed_direct))
     top, bottom = own[:half], own[half:]
@@ -301,7 +381,8 @@
     o_bottom = shift(r_bottom, -1)
     sums = partial_sums(plan, me, [(0, [own])], None, weights, 14)
     sums = partial_sums(plan, me, [(3, [l_top, l_bottom]), (1, [r_top, r_bottom])], sums, weights, 18)
-    grads, relay_top, relay_bottom, near = gates(plan, me, sums, (o_top, o_bottom), arrived_direct, weights)
+    sums = near_sums(plan, me, sums, arrived_direct, weights)
+    grads, relay_top, relay_bottom, near = gates(plan, me, sums, (o_top, o_bottom), weights)
 
     o_top = shift(relay_top, 1)
     o_bottom = shift(relay_bottom, -1)
@@ -321,7 +402,10 @@
     total, back_direct = lax.optimization_barrier((total, back_direct))
     back_far = exchange(total)
 
-    spread = choose * jnp.concatenate([weight, weight], axis=0)
+    owner = lax.broadcasted_iota(jnp.int32, (toks, rows), 1) // group
+    hit = routes[:, :, None] == owner[:, None, :]
+    weight = jnp.sum(jnp.where(hit, combine[:, :, None], 0.0), axis=1)
+    spread = select.astype(F32) * jnp.concatenate([weight, weight], axis=0)
     coarse = lax.reduce_precision(spread, 8, 7)
     fine = (spread - coarse).astype(BF16)
     coarse = coarse.astype(BF16)

time: 239 us -> 234 us (0.979)
  Pallas kernels: 26.9 us -> 32 us
  local copies, waits for them, and re-layouts: 7.73 us -> 2.83 us
  starting transfers between devices: 68.7 us -> 65.4 us
    unnamed x15 -> x6, local copies, waits for them, and re-layouts: 5.69 us -> 0.15 us
    pallas_call x6 -> x8, Pallas kernels: 26.9 us -> 32 us  [call(): pl.pallas_call(kernel, in_specs=specs, out_specs=out_specs or [VMEM] * le...]
    ppermute x18, starting transfers between devices: 26.1 us -> 23.2 us  [shift(): lax.ppermute(v, 'hidden', [(i, (i + k) % parts) for i in range(parts)])]
  transfers between devices with their start and end apart: 22 -> 22, of which waited for: 13 -> 14; matrix products, arithmetic and copies ran while one was open for 4% -> 4% of each run, Pallas kernels for 8% -> 9%
where the time goes in v2:
time: 234 us; the launch traced here: 233 us
  waiting for transfers between devices  123 us (53%)
  starting transfers between devices  65.4 us (28%)
  Pallas kernels  32 us (14%)
  matrix products  6.02 us (3%)
  local copies, waits for them, and re-layouts  2.83 us (1%)
  other arithmetic  2.51 us (1%)
    ppermute x18, waiting for transfers between devices, shift(): lax.ppermute(v, 'hidden', [(i, (i + k) % parts) for i in range(parts)])  69.1 us
    all_to_all x4, waiting for transfers between devices, exchange(): lax.all_to_all(v.reshape(sources, group, v.shape[1]), 'expert', split_axi...  54.2 us
    all_to_all x4, starting transfers between devices, exchange(): lax.all_to_all(v.reshape(sources, group, v.shape[1]), 'expert', split_axi...  42.2 us
    pallas_call x8, Pallas kernels, call(): pl.pallas_call(kernel, in_specs=specs, out_specs=out_specs or [VMEM] * le...  32 us
    ppermute x18, starting transfers between devices, shift(): lax.ppermute(v, 'hidden', [(i, (i + k) % parts) for i in range(parts)])  23.2 us
  transfers between devices with their start and end apart: 22, of which 14 were waited for; matrix products, arithmetic and copies ran while one was open for 4% of the time, Pallas kernels for 9%

profile of v2, /device:TPU:1, one launch (start us, length us, event | category | flops | bytes accessed | tf_op | source)
XLA Modules:
  0.0 232.8 jit_solution(17889380032964511449)
XLA Ops:
  3.3 13.0 %all-to-all-start = ((bf16[64,8,1408]{2,1,0:T(8,128)(2,1)}), bf16[64,8,1408]{2,1,0:T(8,128)(2,1)S(1)}, u32[]{:S(2)}, u32[]{:S(2)}) async-start(bf16[64,8,1408]{2,1,0:T(8,128)(2,1)} %bitcast.2), calls=%async_computation | async-start | bytes 2883584 | tf_op jit(solution)/shard_map/all_to_all | solution.py:356
  17.8 2.7 %collective-permute-start = (bf16[32,384]{1,0:T(8,128)(2,1)S(1)}, bf16[32,384]{1,0:T(8,128)(2,1)S(1)}, u32[]{:S(2)}, u32[]{:S(2)}) collective-permute-start(bf16[32,384]{1,0:T(8,128)(2,1)S(1)} %pad_maximum_fusion.1), channel_id=1, source_target_pairs={{0,3},{1,0},{2,1},{3,2},{4,7},{5,4},{6,5},{7,6},{8,11},{9,8},{10,9... | collective-permute-start | bytes 73736 | tf_op jit(solution)/shard_map/ppermute | solution.py:353
  21.5 3.4 %collective-permute-done.1 = bf16[32,384]{1,0:T(8,128)(2,1)S(1)} collective-permute-done((bf16[32,384]{1,0:T(8,128)(2,1)S(1)}, bf16[32,384]{1,0:T(8,128)(2,1)S(1)}, u32[]{:S(2)}, u32[]{:S(2)}) %collective-permute-start.1) | collective-permute-done | bytes 24608 | tf_op jit(solution)/shard_map/ppermute | solution.py:353
  27.0 26.3 %all-to-all-done = bf16[64,8,1408]{2,1,0:T(8,128)(2,1)S(1)} async-done(((bf16[64,8,1408]{2,1,0:T(8,128)(2,1)}), bf16[64,8,1408]{2,1,0:T(8,128)(2,1)S(1)}, u32[]{:S(2)}, u32[]{:S(2)}) %all-to-all-start) | async-done | bytes 1441824 | tf_op jit(solution)/shard_map/all_to_all | solution.py:356
  53.3 6.1 %all-to-all-start.1 = ((bf16[64,8,1536]{2,1,0:T(8,128)(2,1)}), bf16[64,8,1536]{2,1,0:T(8,128)(2,1)S(1)}, u32[]{:S(2)}, u32[]{:S(2)}) async-start(bf16[64,8,1536]{2,1,0:T(8,128)(2,1)} %bitcast.44), calls=%async_computation.1 | async-start | bytes 3145728 | tf_op jit(solution)/shard_map/all_to_all | solution.py:356
  66.1 13.5 %collective-permute-done.3.refs_1_ = bf16[256,1408]{1,0:T(8,128)(2,1)} collective-permute-done((bf16[256,1408]{1,0:T(8,128)(2,1)}, bf16[256,1408]{1,0:T(8,128)(2,1)}, u32[]{:S(2)}, u32[]{:S(2)}) %collective-permute-start.3) | collective-permute-done | bytes 720928 | tf_op jit(solution)/shard_map/ppermute | solution.py:353
  82.2 3.0 %shard_map.87.refs_0_ = f32[512,768]{1,0:T(8,128)S(1)} custom-call(s32[1]{0:T(128)} %bitcast.1.me_ref, bf16[512,1408]{1,0:T(8,128)(2,1)S(1)} %bitcast.21, bf16[7168,256]{1,0:T(8,128)(2,1)} %bitcast.23, bf16[7168,256]{1,0:T(8,128)(2,1)} %bitcast.30, bf16[256,7168]{1,0:T(8,128)(2,1)} %bitcast.37), custom_call_target="tpu_custom_call" | custom-call | flops 1107296256 | bytes 5636096 | tf_op jit(solution)/shard_map/pallas_call | solution.py:73
  85.2 9.8 %collective-permute-done.4.refs_2_ = bf16[256,1408]{1,0:T(8,128)(2,1)} collective-permute-done((bf16[256,1408]{1,0:T(8,128)(2,1)}, bf16[256,1408]{1,0:T(8,128)(2,1)}, u32[]{:S(2)}, u32[]{:S(2)}) %collective-permute-start.4) | collective-permute-done | bytes 720928 | tf_op jit(solution)/shard_map/ppermute | solution.py:353
  95.0 6.1 %shard_map.88.sums_ref = f32[512,768]{1,0:T(8,128)S(1)} custom-call(s32[1]{0:T(128)} %bitcast.1.me_ref, f32[512,768]{1,0:T(8,128)S(1)} %shard_map.87.refs_0_, bf16[256,1408]{1,0:T(8,128)(2,1)} %collective-permute-done.3.refs_1_, bf16[256,1408]{1,0:T(8,128)(2,1)} %collective-permute-done.4.refs_2_, bf16[256,1408]{1,0:T(8,128)(2,1)} %collective-permute-done.5.refs_3_, ...), custom_call_target="tpu_custom_call" | custom-call | flops 2214592512 | bytes 8650752 | tf_op jit(solution)/shard_map/pallas_call | solution.py:73
  101.1 3.2 %shard_map.89.sums_hbm = f32[512,768]{1,0:T(8,128)S(1)} custom-call(s32[1]{0:T(128)} %bitcast.1.me_ref, f32[512,768]{1,0:T(8,128)S(1)} %shard_map.88.sums_ref, bf16[512,1536]{1,0:T(8,128)(2,1)S(1)} %bitcast.22, bf16[7168,256]{1,0:T(8,128)(2,1)} %bitcast.25, bf16[7168,256]{1,0:T(8,128)(2,1)} %bitcast.32, bf16[256,7168]{1,0:T(8,128)(2,1)} %bitcast.39), custom_call_target="tpu_custom_call" | custom-call | flops 1207959552 | bytes 7340032 | tf_op jit(solution)/shard_map/pallas_call | solution.py:73
  104.3 6.1 %collective-permute-done.7.refs_0_ = bf16[256,1408]{1,0:T(8,128)(2,1)} collective-permute-done((bf16[256,1408]{1,0:T(8,128)(2,1)}, bf16[256,1408]{1,0:T(8,128)(2,1)}, u32[]{:S(2)}, u32[]{:S(2)}) %collective-permute-start.7) | collective-permute-done | bytes 720928 | tf_op jit(solution)/shard_map/ppermute | solution.py:353
  110.5 7.5 %shard_map.90 = (bf16[512,768]{1,0:T(8,128)(2,1)S(1)}, bf16[256,1408]{1,0:T(8,128)(2,1)S(1)}, bf16[256,1408]{1,0:T(8,128)(2,1)S(1)}, bf16[512,1536]{1,0:T(8,128)(2,1)}) custom-call(s32[1]{0:T(128)} %bitcast.1.me_ref, f32[512,768]{1,0:T(8,128)S(1)} %shard_map.89.sums_hbm, bf16[256,1408]{1,0:T(8,128)(2,1)} %collective-permute-done.7.refs_0_, ...), custom_call_target="tpu_custom_call" | custom-call | flops 3422552064 | bytes 4194304 | tf_op jit(solution)/shard_map/pallas_call | solution.py:73
  118.0 11.4 %all-to-all-start.2 = ((bf16[64,8,1536]{2,1,0:T(8,128)(2,1)}), bf16[64,8,1536]{2,1,0:T(8,128)(2,1)}, u32[]{:S(2)}, u32[]{:S(2)}) async-start(bf16[64,8,1536]{2,1,0:T(8,128)(2,1)} %bitcast.45), calls=%async_computation.2 | async-start | bytes 3145728 | tf_op jit(solution)/shard_map/all_to_all | solution.py:356
  129.4 2.7 %collective-permute-start.10 = (bf16[256,1408]{1,0:T(8,128)(2,1)S(1)}, bf16[256,1408]{1,0:T(8,128)(2,1)S(1)}, u32[]{:S(2)}, u32[]{:S(2)}) collective-permute-start(bf16[256,1408]{1,0:T(8,128)(2,1)S(1)} %get-tuple-element.22), channel_id=1, source_target_pairs={{0,3},{1,0},{2,1},{3,2},{4,7},{5,4},{6,5},{7,6},{8,11},{9,8},{10,9... | collective-permute-start | bytes 2162696 | tf_op jit(solution)/shard_map/ppermute | solution.py:353
  132.1 3.2 %shard_map.93 = (bf16[256,1408]{1,0:T(8,128)(2,1)S(1)}, bf16[256,1408]{1,0:T(8,128)(2,1)S(1)}) custom-call(s32[1]{0:T(128)} %bitcast.1.me_ref, bf16[512,768]{1,0:T(8,128)(2,1)S(1)} %get-tuple-element.20.h_ref, bf16[7168,256]{1,0:T(8,128)(2,1)} %bitcast.27, bf16[7168,256]{1,0:T(8,128)(2,1)} %bitcast.34, bf16[256,7168]{1,0:T(8,128)(2,1)} %bitcast.41), custom_call_target="tpu_custom_call" | custom-call | flops 1107296256 | bytes 4980736 | tf_op jit(solution)/shard_map/pallas_call | solution.py:73
  135.6 2.9 %collective-permute-start.13 = (bf16[256,1408]{1,0:T(8,128)(2,1)S(1)}, bf16[256,1408]{1,0:T(8,128)(2,1)S(1)}, u32[]{:S(2)}, u32[]{:S(2)}) collective-permute-start(bf16[256,1408]{1,0:T(8,128)(2,1)S(1)} %get-tuple-element.25), channel_id=1, source_target_pairs={{0,3},{1,0},{2,1},{3,2},{4,7},{5,4},{6,5},{7,6},{8,11},{9,8},{10,9... | collective-permute-start | bytes 2162696 | tf_op jit(solution)/shard_map/ppermute | solution.py:353
  138.4 8.7 %collective-permute-done.10.refs_1_ = bf16[256,1408]{1,0:T(8,128)(2,1)S(1)} collective-permute-done((bf16[256,1408]{1,0:T(8,128)(2,1)S(1)}, bf16[256,1408]{1,0:T(8,128)(2,1)S(1)}, u32[]{:S(2)}, u32[]{:S(2)}) %collective-permute-start.10) | collective-permute-done | bytes 720928 | tf_op jit(solution)/shard_map/ppermute | solution.py:353
  147.1 3.2 %collective-permute-done.9.refs_0_ = bf16[256,1408]{1,0:T(8,128)(2,1)S(1)} collective-permute-done((bf16[256,1408]{1,0:T(8,128)(2,1)S(1)}, bf16[256,1408]{1,0:T(8,128)(2,1)S(1)}, u32[]{:S(2)}, u32[]{:S(2)}) %collective-permute-start.9) | collective-permute-done | bytes 720928 | tf_op jit(solution)/shard_map/ppermute | solution.py:353
  150.3 3.2 %shard_map.92 = (bf16[256,1408]{1,0:T(8,128)(2,1)S(1)}, bf16[256,1408]{1,0:T(8,128)(2,1)S(1)}) custom-call(s32[1]{0:T(128)} %bitcast.1.me_ref, bf16[512,768]{1,0:T(8,128)(2,1)S(1)} %get-tuple-element.20.h_ref, bf16[256,1408]{1,0:T(8,128)(2,1)S(1)} %collective-permute-done.9.refs_0_, bf16[256,1408]{1,0:T(8,128)(2,1)S(1)} %collective-permute-done.10.refs_1_, ...), custom_call_target="tpu_custom_call" | custom-call | flops 1107296256 | bytes 6422528 | tf_op jit(solution)/shard_map/pallas_call | solution.py:73
  156.3 3.0 %shard_map.91 = bf16[512,1408]{1,0:T(8,128)(2,1)S(1)} custom-call(s32[1]{0:T(128)} %bitcast.1.me_ref, bf16[512,768]{1,0:T(8,128)(2,1)S(1)} %get-tuple-element.20.h_ref, bf16[7168,256]{1,0:T(8,128)(2,1)} %bitcast.29, bf16[7168,256]{1,0:T(8,128)(2,1)} %bitcast.36, bf16[256,7168]{1,0:T(8,128)(2,1)} %bitcast.43), custom_call_target="tpu_custom_call" | custom-call | flops 1107296256 | bytes 4980736 | tf_op jit(solution)/shard_map/pallas_call | solution.py:73
  159.3 6.5 %collective-permute-done.12 = bf16[256,1408]{1,0:T(8,128)(2,1)S(1)} collective-permute-done((bf16[256,1408]{1,0:T(8,128)(2,1)S(1)}, bf16[256,1408]{1,0:T(8,128)(2,1)S(1)}, u32[]{:S(2)}, u32[]{:S(2)}) %collective-permute-start.12) | collective-permute-done | bytes 720928 | tf_op jit(solution)/shard_map/ppermute | solution.py:353
  165.8 15.3 %collective-permute-done.11 = bf16[256,1408]{1,0:T(8,128)(2,1)S(1)} collective-permute-done((bf16[256,1408]{1,0:T(8,128)(2,1)S(1)}, bf16[256,1408]{1,0:T(8,128)(2,1)S(1)}, u32[]{:S(2)}, u32[]{:S(2)}) %collective-permute-start.11) | collective-permute-done | bytes 720928 | tf_op jit(solution)/shard_map/ppermute | solution.py:353
  182.8 11.7 %all-to-all-start.3 = ((bf16[64,8,1408]{2,1,0:T(8,128)(2,1)}), bf16[64,8,1408]{2,1,0:T(8,128)(2,1)S(1)}, u32[]{:S(2)}, u32[]{:S(2)}) async-start(bf16[64,8,1408]{2,1,0:T(8,128)(2,1)} %bitcast.11), calls=%async_computation.3 | async-start | bytes 2883584 | tf_op jit(solution)/shard_map/all_to_all | solution.py:356
  203.6 27.9 %all-to-all-done.3 = bf16[64,8,1408]{2,1,0:T(8,128)(2,1)S(1)} async-done(((bf16[64,8,1408]{2,1,0:T(8,128)(2,1)}), bf16[64,8,1408]{2,1,0:T(8,128)(2,1)S(1)}, u32[]{:S(2)}, u32[]{:S(2)}) %all-to-all-start.3) | async-done | bytes 1441824 | tf_op jit(solution)/shard_map/all_to_all | solution.py:356
  (51 shorter events, 31.5 us)
Async XLA Ops:
  3.3 49.9 %all-to-all-start = ((bf16[64,8,1408]{2,1,0:T(8,128)(2,1)}), bf16[64,8,1408]{2,1,0:T(8,128)(2,1)S(1)}, u32[]{:S(2)}, u32[]{:S(2)}) async-start(bf16[64,8,1408]{2,1,0:T(8,128)(2,1)} %bitcast.2), calls=%async_computation | async-start | bytes 2883584 | tf_op jit(solution)/shard_map/all_to_all | solution.py:356
  17.8 3.8 %collective-permute-start = (bf16[32,384]{1,0:T(8,128)(2,1)S(1)}, bf16[32,384]{1,0:T(8,128)(2,1)S(1)}, u32[]{:S(2)}, u32[]{:S(2)}) collective-permute-start(bf16[32,384]{1,0:T(8,128)(2,1)S(1)} %pad_maximum_fusion.1), channel_id=1, source_target_pairs={{0,3},{1,0},{2,1},{3,2},{4,7},{5,4},{6,5},{7,6},{8,11},{9,8},{10,9... | collective-permute-start | bytes 73736 | tf_op jit(solution)/shard_map/ppermute | solution.py:353
  20.5 4.5 %collective-permute-start.1 = (bf16[32,384]{1,0:T(8,128)(2,1)S(1)}, bf16[32,384]{1,0:T(8,128)(2,1)S(1)}, u32[]{:S(2)}, u32[]{:S(2)}) collective-permute-start(bf16[32,384]{1,0:T(8,128)(2,1)S(1)} %pad_maximum_fusion.1), channel_id=1, source_target_pairs={{0,2},{1,3},{2,0},{3,1},{4,6},{5,7},{6,4},{7,5},{8,10},{9,11},{10,... | collective-permute-start | bytes 73736 | tf_op jit(solution)/shard_map/ppermute | solution.py:353
  20.8 4.4 %collective-permute-start.2 = (bf16[32,384]{1,0:T(8,128)(2,1)S(1)}, bf16[32,384]{1,0:T(8,128)(2,1)S(1)}, u32[]{:S(2)}, u32[]{:S(2)}) collective-permute-start(bf16[32,384]{1,0:T(8,128)(2,1)S(1)} %pad_maximum_fusion.1), channel_id=1, source_target_pairs={{0,1},{1,2},{2,3},{3,0},{4,5},{5,6},{6,7},{7,4},{8,9},{9,10},{10,1... | collective-permute-start | bytes 73736 | tf_op jit(solution)/shard_map/ppermute | solution.py:353
  53.3 47.9 %all-to-all-start.1 = ((bf16[64,8,1536]{2,1,0:T(8,128)(2,1)}), bf16[64,8,1536]{2,1,0:T(8,128)(2,1)S(1)}, u32[]{:S(2)}, u32[]{:S(2)}) async-start(bf16[64,8,1536]{2,1,0:T(8,128)(2,1)} %bitcast.44), calls=%async_computation.1 | async-start | bytes 3145728 | tf_op jit(solution)/shard_map/all_to_all | solution.py:356
  60.7 18.9 %collective-permute-start.3 = (bf16[256,1408]{1,0:T(8,128)(2,1)}, bf16[256,1408]{1,0:T(8,128)(2,1)}, u32[]{:S(2)}, u32[]{:S(2)}) collective-permute-start(bf16[256,1408]{1,0:T(8,128)(2,1)} %get-tuple-element.31), channel_id=1, source_target_pairs={{0,1},{1,2},{2,3},{3,0},{4,5},{5,6},{6,7},{7,4},{8,9},{9,10},{10,1... | collective-permute-start | bytes 2162696 | tf_op jit(solution)/shard_map/ppermute | solution.py:353
  62.0 17.6 %collective-permute-start.6 = (bf16[256,1408]{1,0:T(8,128)(2,1)}, bf16[256,1408]{1,0:T(8,128)(2,1)}, u32[]{:S(2)}, u32[]{:S(2)}) collective-permute-start(bf16[256,1408]{1,0:T(8,128)(2,1)} %get-tuple-element.30), channel_id=1, source_target_pairs={{0,3},{1,0},{2,1},{3,2},{4,7},{5,4},{6,5},{7,6},{8,11},{9,8},{10,9... | collective-permute-start | bytes 2162696 | tf_op jit(solution)/shard_map/ppermute | solution.py:353
  63.4 31.6 %collective-permute-start.4 = (bf16[256,1408]{1,0:T(8,128)(2,1)}, bf16[256,1408]{1,0:T(8,128)(2,1)}, u32[]{:S(2)}, u32[]{:S(2)}) collective-permute-start(bf16[256,1408]{1,0:T(8,128)(2,1)} %get-tuple-element.30), channel_id=1, source_target_pairs={{0,1},{1,2},{2,3},{3,0},{4,5},{5,6},{6,7},{7,4},{8,9},{9,10},{10,1... | collective-permute-start | bytes 2162696 | tf_op jit(solution)/shard_map/ppermute | solution.py:353
  63.4 31.6 %collective-permute-start.5 = (bf16[256,1408]{1,0:T(8,128)(2,1)}, bf16[256,1408]{1,0:T(8,128)(2,1)}, u32[]{:S(2)}, u32[]{:S(2)}) collective-permute-start(bf16[256,1408]{1,0:T(8,128)(2,1)} %get-tuple-element.31), channel_id=1, source_target_pairs={{0,3},{1,0},{2,1},{3,2},{4,7},{5,4},{6,5},{7,6},{8,11},{9,8},{10,9... | collective-permute-start | bytes 2162696 | tf_op jit(solution)/shard_map/ppermute | solution.py:353
  79.6 30.9 %collective-permute-start.7 = (bf16[256,1408]{1,0:T(8,128)(2,1)}, bf16[256,1408]{1,0:T(8,128)(2,1)}, u32[]{:S(2)}, u32[]{:S(2)}) collective-permute-start(bf16[256,1408]{1,0:T(8,128)(2,1)} %collective-permute-done.3.refs_1_), channel_id=1, source_target_pairs={{0,1},{1,2},{2,3},{3,0},{4,5},{5,6},{6,7},{7,4},{8,9},{9,10},{10,1... | collective-permute-start | bytes 2162696 | tf_op jit(solution)/shard_map/ppermute | solution.py:353
  79.6 30.9 %collective-permute-start.8 = (bf16[256,1408]{1,0:T(8,128)(2,1)}, bf16[256,1408]{1,0:T(8,128)(2,1)}, u32[]{:S(2)}, u32[]{:S(2)}) collective-permute-start(bf16[256,1408]{1,0:T(8,128)(2,1)} %collective-permute-done.6.refs_4_), channel_id=1, source_target_pairs={{0,3},{1,0},{2,1},{3,2},{4,7},{5,4},{6,5},{7,6},{8,11},{9,8},{10,9... | collective-permute-start | bytes 2162696 | tf_op jit(solution)/shard_map/ppermute | solution.py:353
  118.0 64.8 %all-to-all-start.2 = ((bf16[64,8,1536]{2,1,0:T(8,128)(2,1)}), bf16[64,8,1536]{2,1,0:T(8,128)(2,1)}, u32[]{:S(2)}, u32[]{:S(2)}) async-start(bf16[64,8,1536]{2,1,0:T(8,128)(2,1)} %bitcast.45), calls=%async_computation.2 | async-start | bytes 3145728 | tf_op jit(solution)/shard_map/all_to_all | solution.py:356
  129.4 17.7 %collective-permute-start.10 = (bf16[256,1408]{1,0:T(8,128)(2,1)S(1)}, bf16[256,1408]{1,0:T(8,128)(2,1)S(1)}, u32[]{:S(2)}, u32[]{:S(2)}) collective-permute-start(bf16[256,1408]{1,0:T(8,128)(2,1)S(1)} %get-tuple-element.22), channel_id=1, source_target_pairs={{0,3},{1,0},{2,1},{3,2},{4,7},{5,4},{6,5},{7,6},{8,11},{9,8},{10,9... | collective-permute-start | bytes 2162696 | tf_op jit(solution)/shard_map/ppermute | solution.py:353
  132.1 18.2 %collective-permute-start.9 = (bf16[256,1408]{1,0:T(8,128)(2,1)S(1)}, bf16[256,1408]{1,0:T(8,128)(2,1)S(1)}, u32[]{:S(2)}, u32[]{:S(2)}) collective-permute-start(bf16[256,1408]{1,0:T(8,128)(2,1)S(1)} %get-tuple-element.21), channel_id=1, source_target_pairs={{0,1},{1,2},{2,3},{3,0},{4,5},{5,6},{6,7},{7,4},{8,9},{9,10},{10,1... | collective-permute-start | bytes 2162696 | tf_op jit(solution)/shard_map/ppermute | solution.py:353
  135.4 30.4 %collective-permute-start.12 = (bf16[256,1408]{1,0:T(8,128)(2,1)S(1)}, bf16[256,1408]{1,0:T(8,128)(2,1)S(1)}, u32[]{:S(2)}, u32[]{:S(2)}) collective-permute-start(bf16[256,1408]{1,0:T(8,128)(2,1)S(1)} %get-tuple-element.24), channel_id=1, source_target_pairs={{0,1},{1,2},{2,3},{3,0},{4,5},{5,6},{6,7},{7,4},{8,9},{9,10},{10,1... | collective-permute-start | bytes 2162696 | tf_op jit(solution)/shard_map/ppermute | solution.py:353
  135.6 30.2 %collective-permute-start.13 = (bf16[256,1408]{1,0:T(8,128)(2,1)S(1)}, bf16[256,1408]{1,0:T(8,128)(2,1)S(1)}, u32[]{:S(2)}, u32[]{:S(2)}) collective-permute-start(bf16[256,1408]{1,0:T(8,128)(2,1)S(1)} %get-tuple-element.25), channel_id=1, source_target_pairs={{0,3},{1,0},{2,1},{3,2},{4,7},{5,4},{6,5},{7,6},{8,11},{9,8},{10,9... | collective-permute-start | bytes 2162696 | tf_op jit(solution)/shard_map/ppermute | solution.py:353
  153.6 27.6 %collective-permute-start.11 = (bf16[256,1408]{1,0:T(8,128)(2,1)S(1)}, bf16[256,1408]{1,0:T(8,128)(2,1)S(1)}, u32[]{:S(2)}, u32[]{:S(2)}) collective-permute-start(bf16[256,1408]{1,0:T(8,128)(2,1)S(1)} %get-tuple-element.23), channel_id=1, source_target_pairs={{0,1},{1,2},{2,3},{3,0},{4,5},{5,6},{6,7},{7,4},{8,9},{9,10},{10,1... | collective-permute-start | bytes 2162696 | tf_op jit(solution)/shard_map/ppermute | solution.py:353
  153.7 27.5 %collective-permute-start.14 = (bf16[256,1408]{1,0:T(8,128)(2,1)S(1)}, bf16[256,1408]{1,0:T(8,128)(2,1)S(1)}, u32[]{:S(2)}, u32[]{:S(2)}) collective-permute-start(bf16[256,1408]{1,0:T(8,128)(2,1)S(1)} %get-tuple-element.26), channel_id=1, source_target_pairs={{0,3},{1,0},{2,1},{3,2},{4,7},{5,4},{6,5},{7,6},{8,11},{9,8},{10,9... | collective-permute-start | bytes 2162696 | tf_op jit(solution)/shard_map/ppermute | solution.py:353
  182.8 11.7 %copy-start = (s32[16,8]{0,1:T(8,128)S(1)}, s32[16,8]{0,1:T(8,128)}, u32[]{:S(2)}) copy-start(s32[16,8]{0,1:T(8,128)} %param.8) | copy-start | bytes 1540
  182.8 11.8 %copy-start.1 = (f32[16,8]{0,1:T(8,128)S(1)}, f32[16,8]{0,1:T(8,128)}, u32[]{:S(2)}) copy-start(f32[16,8]{0,1:T(8,128)} %param.9) | copy-start | bytes 1540
  182.8 48.7 %all-to-all-start.3 = ((bf16[64,8,1408]{2,1,0:T(8,128)(2,1)}), bf16[64,8,1408]{2,1,0:T(8,128)(2,1)S(1)}, u32[]{:S(2)}, u32[]{:S(2)}) async-start(bf16[64,8,1408]{2,1,0:T(8,128)(2,1)} %bitcast.11), calls=%async_computation.3 | async-start | bytes 2883584 | tf_op jit(solution)/shard_map/all_to_all | solution.py:356
  198.4 4.3 %collective-permute-start.15 = (bf16[32,384]{1,0:T(8,128)(2,1)S(1)}, bf16[32,384]{1,0:T(8,128)(2,1)S(1)}, u32[]{:S(2)}, u32[]{:S(2)}) collective-permute-start(bf16[32,384]{1,0:T(8,128)(2,1)S(1)} %get-tuple-element.34), channel_id=1, source_target_pairs={{0,1},{1,2},{2,3},{3,0},{4,5},{5,6},{6,7},{7,4},{8,9},{9,10},{10,1... | collective-permute-start | bytes 73736 | tf_op jit(solution)/shard_map/ppermute | solution.py:353
  198.5 4.6 %collective-permute-start.16 = (bf16[32,384]{1,0:T(8,128)(2,1)S(1)}, bf16[32,384]{1,0:T(8,128)(2,1)S(1)}, u32[]{:S(2)}, u32[]{:S(2)}) collective-permute-start(bf16[32,384]{1,0:T(8,128)(2,1)S(1)} %get-tuple-element.36), channel_id=1, source_target_pairs={{0,2},{1,3},{2,0},{3,1},{4,6},{5,7},{6,4},{7,5},{8,10},{9,11},{10,... | collective-permute-start | bytes 73736 | tf_op jit(solution)/shard_map/ppermute | solution.py:353
  199.7 3.8 %collective-permute-start.17 = (bf16[32,384]{1,0:T(8,128)(2,1)S(1)}, bf16[32,384]{1,0:T(8,128)(2,1)S(1)}, u32[]{:S(2)}, u32[]{:S(2)}) collective-permute-start(bf16[32,384]{1,0:T(8,128)(2,1)S(1)} %get-tuple-element.35), channel_id=1, source_target_pairs={{0,3},{1,0},{2,1},{3,2},{4,7},{5,4},{6,5},{7,6},{8,11},{9,8},{10,9... | collective-permute-start | bytes 73736 | tf_op jit(solution)/shard_map/ppermute | solution.py:353

commit v3 on v2

--- a/solution.py
+++ b/solution.py
@@ -15,6 +15,7 @@
 HBM = pl.BlockSpec(memory_space=pltpu.HBM)
 SMEM = pl.BlockSpec(memory_space=pltpu.SMEM)
 VMEM = pl.BlockSpec(memory_space=pltpu.VMEM)
+KEPT = pl.BlockSpec(memory_space=pltpu.VMEM)
 
 
 def dot(a, b):
@@ -75,7 +76,7 @@
         in_specs=specs,
         out_specs=out_specs or [VMEM] * len(outs),
         out_shape=[
-            pltpu.HBM(s, t) if spec is HBM else jax.ShapeDtypeStruct(s, t)
+            pltpu.HBM(s, t) if spec is HBM else pltpu.VMEM(s, t) if spec is KEPT else jax.ShapeDtypeStruct(s, t)
             for (s, t), spec in zip(outs, out_specs or [VMEM] * len(outs))
         ],
         scratch_shapes=scratch,
@@ -214,14 +215,14 @@
                 [pltpu.make_async_copy(x_hbm[2 * i + j], x_buf.at[2 * i + j], x_sems.at[2 * i + j]) for j in range(2)]
             )
             loads.append(weight_loads + x_loads)
-        near_loads = [
-            c
-            for k in range(plan.parts)
-            for c in run(plan.copies(me_ref, k, 0, DIRECT, hbm, near, n_sems.at[k], k * DIRECT))
-        ]
         first_load.wait()
         for i in range(n):
             done(loads[i])
+            near_loads = [
+                c
+                for k in range(plan.parts)
+                for c in run(plan.copies(me_ref, k, 0, DIRECT, hbm, near, n_sems.at[k], k * DIRECT))
+            ]
             for j in range(2):
                 for t, term in enumerate(forward(x_buf[2 * i + j], far[3 * i : 3 * i + 3])):
                     acc[j * half : (j + 1) * half, t * w : (t + 1) * w] += term
@@ -274,7 +275,7 @@
         [SMEM] + [ANY] * (2 * n + 1) + [HBM] * 3,
         2 * rows * 3 * w * ((n + 1) * plan.far + near_cols),
         26,
-        [VMEM, VMEM, VMEM, HBM],
+        [VMEM, KEPT, KEPT, HBM],
     )
     return out
 
@@ -283,8 +284,8 @@
     rows, w = sums.shape[0], plan.width
     near_cols = plan.parts * DIRECT
 
-    def kernel(me_ref, sums_ref, x_ref, wg, wu, wd, out_ref, g, u, d, sems):
-        loads = []
+    def kernel(me_ref, sums_ref, x_hbm, wg, wu, wd, out_ref, x_ref, g, u, d, sems, x_sem):
+        loads = run([pltpu.make_async_copy(x_hbm, x_ref, x_sem.at[0])])
         for k in range(plan.parts):
             loads += run(plan.copies(me_ref, k, 0, DIRECT, (wg, wu, wd), (g, u, d), sems.at[k], k * DIRECT))
         done(loads)
@@ -296,8 +297,10 @@
         kernel,
         [((rows, 3 * w), F32)],
         (me, sums, direct, *weights),
-        plan.weight_scratch(near_cols) + [pltpu.SemaphoreType.DMA((plan.parts, 3))],
-        [SMEM, VMEM, VMEM, HBM, HBM, HBM],
+        [pltpu.VMEM((rows, near_cols), BF16)]
+        + plan.weight_scratch(near_cols)
+        + [pltpu.SemaphoreType.DMA((plan.parts, 3)), pltpu.SemaphoreType.DMA((1,))],
+        [SMEM, VMEM, ANY, HBM, HBM, HBM],
         2 * rows * 3 * w * near_cols,
         16,
     )[0]

time: 234 us -> 234 us (level)
  no operation moved by 1% of the time
where the time goes in v3:
time: 234 us; the launch traced here: 233 us
  waiting for transfers between devices  123 us (53%)
  starting transfers between devices  65.4 us (28%)
  Pallas kernels  32.3 us (14%)
  matrix products  6.02 us (3%)
  local copies, waits for them, and re-layouts  2.83 us (1%)
  other arithmetic  2.51 us (1%)
    ppermute x18, waiting for transfers between devices, shift(): lax.ppermute(v, 'hidden', [(i, (i + k) % parts) for i in range(parts)])  69 us
    all_to_all x4, waiting for transfers between devices, exchange(): lax.all_to_all(v.reshape(sources, group, v.shape[1]), 'expert', split_axi...  54.2 us
    all_to_all x4, starting transfers between devices, exchange(): lax.all_to_all(v.reshape(sources, group, v.shape[1]), 'expert', split_axi...  42.2 us
    pallas_call x8, Pallas kernels, call(): pl.pallas_call(kernel, in_specs=specs, out_specs=out_specs or [VMEM] * le...  32.3 us
    ppermute x18, starting transfers between devices, shift(): lax.ppermute(v, 'hidden', [(i, (i + k) % parts) for i in range(parts)])  23.2 us
  transfers between devices with their start and end apart: 22, of which 14 were waited for; matrix products, arithmetic and copies ran while one was open for 4% of the time, Pallas kernels for 9%

profile of v3, /device:TPU:1, one launch (start us, length us, event | category | flops | bytes accessed | tf_op | source)
XLA Modules:
  0.0 233.1 jit_solution(452643746712886655)
XLA Ops:
  3.3 13.0 %all-to-all-start = ((bf16[64,8,1408]{2,1,0:T(8,128)(2,1)}), bf16[64,8,1408]{2,1,0:T(8,128)(2,1)S(1)}, u32[]{:S(2)}, u32[]{:S(2)}) async-start(bf16[64,8,1408]{2,1,0:T(8,128)(2,1)} %bitcast.2), calls=%async_computation | async-start | bytes 2883584 | tf_op jit(solution)/shard_map/all_to_all | solution.py:359
  17.8 2.7 %collective-permute-start = (bf16[32,384]{1,0:T(8,128)(2,1)S(1)}, bf16[32,384]{1,0:T(8,128)(2,1)S(1)}, u32[]{:S(2)}, u32[]{:S(2)}) collective-permute-start(bf16[32,384]{1,0:T(8,128)(2,1)S(1)} %pad_maximum_fusion.1), channel_id=1, source_target_pairs={{0,3},{1,0},{2,1},{3,2},{4,7},{5,4},{6,5},{7,6},{8,11},{9,8},{10,9... | collective-permute-start | bytes 73736 | tf_op jit(solution)/shard_map/ppermute | solution.py:356
  21.5 3.4 %collective-permute-done.1 = bf16[32,384]{1,0:T(8,128)(2,1)S(1)} collective-permute-done((bf16[32,384]{1,0:T(8,128)(2,1)S(1)}, bf16[32,384]{1,0:T(8,128)(2,1)S(1)}, u32[]{:S(2)}, u32[]{:S(2)}) %collective-permute-start.1) | collective-permute-done | bytes 24608 | tf_op jit(solution)/shard_map/ppermute | solution.py:356
  27.0 26.3 %all-to-all-done = bf16[64,8,1408]{2,1,0:T(8,128)(2,1)S(1)} async-done(((bf16[64,8,1408]{2,1,0:T(8,128)(2,1)}), bf16[64,8,1408]{2,1,0:T(8,128)(2,1)S(1)}, u32[]{:S(2)}, u32[]{:S(2)}) %all-to-all-start) | async-done | bytes 1441824 | tf_op jit(solution)/shard_map/all_to_all | solution.py:359
  53.3 6.1 %all-to-all-start.1 = ((bf16[64,8,1536]{2,1,0:T(8,128)(2,1)}), bf16[64,8,1536]{2,1,0:T(8,128)(2,1)S(1)}, u32[]{:S(2)}, u32[]{:S(2)}) async-start(bf16[64,8,1536]{2,1,0:T(8,128)(2,1)} %bitcast.44), calls=%async_computation.1 | async-start | bytes 3145728 | tf_op jit(solution)/shard_map/all_to_all | solution.py:359
  66.1 13.5 %collective-permute-done.3.refs_1_ = bf16[256,1408]{1,0:T(8,128)(2,1)} collective-permute-done((bf16[256,1408]{1,0:T(8,128)(2,1)}, bf16[256,1408]{1,0:T(8,128)(2,1)}, u32[]{:S(2)}, u32[]{:S(2)}) %collective-permute-start.3) | collective-permute-done | bytes 720928 | tf_op jit(solution)/shard_map/ppermute | solution.py:356
  82.2 3.0 %shard_map.87.refs_0_ = f32[512,768]{1,0:T(8,128)S(1)} custom-call(s32[1]{0:T(128)} %bitcast.1.me_ref, bf16[512,1408]{1,0:T(8,128)(2,1)S(1)} %bitcast.21, bf16[7168,256]{1,0:T(8,128)(2,1)} %bitcast.23, bf16[7168,256]{1,0:T(8,128)(2,1)} %bitcast.30, bf16[256,7168]{1,0:T(8,128)(2,1)} %bitcast.37), custom_call_target="tpu_custom_call" | custom-call | flops 1107296256 | bytes 5636096 | tf_op jit(solution)/shard_map/pallas_call | solution.py:74
  85.2 9.8 %collective-permute-done.4.refs_2_ = bf16[256,1408]{1,0:T(8,128)(2,1)} collective-permute-done((bf16[256,1408]{1,0:T(8,128)(2,1)}, bf16[256,1408]{1,0:T(8,128)(2,1)}, u32[]{:S(2)}, u32[]{:S(2)}) %collective-permute-start.4) | collective-permute-done | bytes 720928 | tf_op jit(solution)/shard_map/ppermute | solution.py:356
  95.0 6.1 %shard_map.88.sums_ref = f32[512,768]{1,0:T(8,128)S(1)} custom-call(s32[1]{0:T(128)} %bitcast.1.me_ref, f32[512,768]{1,0:T(8,128)S(1)} %shard_map.87.refs_0_, bf16[256,1408]{1,0:T(8,128)(2,1)} %collective-permute-done.3.refs_1_, bf16[256,1408]{1,0:T(8,128)(2,1)} %collective-permute-done.4.refs_2_, bf16[256,1408]{1,0:T(8,128)(2,1)} %collective-permute-done.5.refs_3_, ...), custom_call_target="tpu_custom_call" | custom-call | flops 2214592512 | bytes 8650752 | tf_op jit(solution)/shard_map/pallas_call | solution.py:74
  101.1 3.3 %shard_map.89.sums_hbm = f32[512,768]{1,0:T(8,128)S(1)} custom-call(s32[1]{0:T(128)} %bitcast.1.me_ref, f32[512,768]{1,0:T(8,128)S(1)} %shard_map.88.sums_ref, bf16[512,1536]{1,0:T(8,128)(2,1)S(1)} %bitcast.22, bf16[7168,256]{1,0:T(8,128)(2,1)} %bitcast.25, bf16[7168,256]{1,0:T(8,128)(2,1)} %bitcast.32, bf16[256,7168]{1,0:T(8,128)(2,1)} %bitcast.39), custom_call_target="tpu_custom_call" | custom-call | flops 1207959552 | bytes 5767168 | tf_op jit(solution)/shard_map/pallas_call | solution.py:74
  104.5 6.0 %collective-permute-done.7.refs_0_ = bf16[256,1408]{1,0:T(8,128)(2,1)} collective-permute-done((bf16[256,1408]{1,0:T(8,128)(2,1)}, bf16[256,1408]{1,0:T(8,128)(2,1)}, u32[]{:S(2)}, u32[]{:S(2)}) %collective-permute-start.7) | collective-permute-done | bytes 720928 | tf_op jit(solution)/shard_map/ppermute | solution.py:356
  110.5 7.8 %shard_map.90 = (bf16[512,768]{1,0:T(8,128)(2,1)S(1)}, bf16[256,1408]{1,0:T(8,128)(2,1)S(1)}, bf16[256,1408]{1,0:T(8,128)(2,1)S(1)}, bf16[512,1536]{1,0:T(8,128)(2,1)}) custom-call(s32[1]{0:T(128)} %bitcast.1.me_ref, f32[512,768]{1,0:T(8,128)S(1)} %shard_map.89.sums_hbm, bf16[256,1408]{1,0:T(8,128)(2,1)} %collective-permute-done.7.refs_0_, ...), custom_call_target="tpu_custom_call" | custom-call | flops 3422552064 | bytes 4194304 | tf_op jit(solution)/shard_map/pallas_call | solution.py:74
  118.3 11.4 %all-to-all-start.2 = ((bf16[64,8,1536]{2,1,0:T(8,128)(2,1)}), bf16[64,8,1536]{2,1,0:T(8,128)(2,1)}, u32[]{:S(2)}, u32[]{:S(2)}) async-start(bf16[64,8,1536]{2,1,0:T(8,128)(2,1)} %bitcast.45), calls=%async_computation.2 | async-start | bytes 3145728 | tf_op jit(solution)/shard_map/all_to_all | solution.py:359
  129.7 2.7 %collective-permute-start.10 = (bf16[256,1408]{1,0:T(8,128)(2,1)S(1)}, bf16[256,1408]{1,0:T(8,128)(2,1)S(1)}, u32[]{:S(2)}, u32[]{:S(2)}) collective-permute-start(bf16[256,1408]{1,0:T(8,128)(2,1)S(1)} %get-tuple-element.22), channel_id=1, source_target_pairs={{0,3},{1,0},{2,1},{3,2},{4,7},{5,4},{6,5},{7,6},{8,11},{9,8},{10,9... | collective-permute-start | bytes 2162696 | tf_op jit(solution)/shard_map/ppermute | solution.py:356
  132.4 3.2 %shard_map.93 = (bf16[256,1408]{1,0:T(8,128)(2,1)S(1)}, bf16[256,1408]{1,0:T(8,128)(2,1)S(1)}) custom-call(s32[1]{0:T(128)} %bitcast.1.me_ref, bf16[512,768]{1,0:T(8,128)(2,1)S(1)} %get-tuple-element.20.h_ref, bf16[7168,256]{1,0:T(8,128)(2,1)} %bitcast.27, bf16[7168,256]{1,0:T(8,128)(2,1)} %bitcast.34, bf16[256,7168]{1,0:T(8,128)(2,1)} %bitcast.41), custom_call_target="tpu_custom_call" | custom-call | flops 1107296256 | bytes 4980736 | tf_op jit(solution)/shard_map/pallas_call | solution.py:74
  135.8 2.9 %collective-permute-start.13 = (bf16[256,1408]{1,0:T(8,128)(2,1)S(1)}, bf16[256,1408]{1,0:T(8,128)(2,1)S(1)}, u32[]{:S(2)}, u32[]{:S(2)}) collective-permute-start(bf16[256,1408]{1,0:T(8,128)(2,1)S(1)} %get-tuple-element.25), channel_id=1, source_target_pairs={{0,3},{1,0},{2,1},{3,2},{4,7},{5,4},{6,5},{7,6},{8,11},{9,8},{10,9... | collective-permute-start | bytes 2162696 | tf_op jit(solution)/shard_map/ppermute | solution.py:356
  138.7 8.7 %collective-permute-done.10.refs_1_ = bf16[256,1408]{1,0:T(8,128)(2,1)S(1)} collective-permute-done((bf16[256,1408]{1,0:T(8,128)(2,1)S(1)}, bf16[256,1408]{1,0:T(8,128)(2,1)S(1)}, u32[]{:S(2)}, u32[]{:S(2)}) %collective-permute-start.10) | collective-permute-done | bytes 720928 | tf_op jit(solution)/shard_map/ppermute | solution.py:356
  147.4 3.2 %collective-permute-done.9.refs_0_ = bf16[256,1408]{1,0:T(8,128)(2,1)S(1)} collective-permute-done((bf16[256,1408]{1,0:T(8,128)(2,1)S(1)}, bf16[256,1408]{1,0:T(8,128)(2,1)S(1)}, u32[]{:S(2)}, u32[]{:S(2)}) %collective-permute-start.9) | collective-permute-done | bytes 720928 | tf_op jit(solution)/shard_map/ppermute | solution.py:356
  150.6 3.2 %shard_map.92 = (bf16[256,1408]{1,0:T(8,128)(2,1)S(1)}, bf16[256,1408]{1,0:T(8,128)(2,1)S(1)}) custom-call(s32[1]{0:T(128)} %bitcast.1.me_ref, bf16[512,768]{1,0:T(8,128)(2,1)S(1)} %get-tuple-element.20.h_ref, bf16[256,1408]{1,0:T(8,128)(2,1)S(1)} %collective-permute-done.9.refs_0_, bf16[256,1408]{1,0:T(8,128)(2,1)S(1)} %collective-permute-done.10.refs_1_, ...), custom_call_target="tpu_custom_call" | custom-call | flops 1107296256 | bytes 6422528 | tf_op jit(solution)/shard_map/pallas_call | solution.py:74
  156.6 3.0 %shard_map.91 = bf16[512,1408]{1,0:T(8,128)(2,1)S(1)} custom-call(s32[1]{0:T(128)} %bitcast.1.me_ref, bf16[512,768]{1,0:T(8,128)(2,1)S(1)} %get-tuple-element.20.h_ref, bf16[7168,256]{1,0:T(8,128)(2,1)} %bitcast.29, bf16[7168,256]{1,0:T(8,128)(2,1)} %bitcast.36, bf16[256,7168]{1,0:T(8,128)(2,1)} %bitcast.43), custom_call_target="tpu_custom_call" | custom-call | flops 1107296256 | bytes 4980736 | tf_op jit(solution)/shard_map/pallas_call | solution.py:74
  159.6 6.5 %collective-permute-done.12 = bf16[256,1408]{1,0:T(8,128)(2,1)S(1)} collective-permute-done((bf16[256,1408]{1,0:T(8,128)(2,1)S(1)}, bf16[256,1408]{1,0:T(8,128)(2,1)S(1)}, u32[]{:S(2)}, u32[]{:S(2)}) %collective-permute-start.12) | collective-permute-done | bytes 720928 | tf_op jit(solution)/shard_map/ppermute | solution.py:356
  166.1 15.3 %collective-permute-done.11 = bf16[256,1408]{1,0:T(8,128)(2,1)S(1)} collective-permute-done((bf16[256,1408]{1,0:T(8,128)(2,1)S(1)}, bf16[256,1408]{1,0:T(8,128)(2,1)S(1)}, u32[]{:S(2)}, u32[]{:S(2)}) %collective-permute-start.11) | collective-permute-done | bytes 720928 | tf_op jit(solution)/shard_map/ppermute | solution.py:356
  183.1 11.7 %all-to-all-start.3 = ((bf16[64,8,1408]{2,1,0:T(8,128)(2,1)}), bf16[64,8,1408]{2,1,0:T(8,128)(2,1)S(1)}, u32[]{:S(2)}, u32[]{:S(2)}) async-start(bf16[64,8,1408]{2,1,0:T(8,128)(2,1)} %bitcast.11), calls=%async_computation.3 | async-start | bytes 2883584 | tf_op jit(solution)/shard_map/all_to_all | solution.py:359
  203.8 27.9 %all-to-all-done.3 = bf16[64,8,1408]{2,1,0:T(8,128)(2,1)S(1)} async-done(((bf16[64,8,1408]{2,1,0:T(8,128)(2,1)}), bf16[64,8,1408]{2,1,0:T(8,128)(2,1)S(1)}, u32[]{:S(2)}, u32[]{:S(2)}) %all-to-all-start.3) | async-done | bytes 1441824 | tf_op jit(solution)/shard_map/all_to_all | solution.py:359
  (51 shorter events, 31.5 us)
Async XLA Ops:
  3.3 49.9 %all-to-all-start = ((bf16[64,8,1408]{2,1,0:T(8,128)(2,1)}), bf16[64,8,1408]{2,1,0:T(8,128)(2,1)S(1)}, u32[]{:S(2)}, u32[]{:S(2)}) async-start(bf16[64,8,1408]{2,1,0:T(8,128)(2,1)} %bitcast.2), calls=%async_computation | async-start | bytes 2883584 | tf_op jit(solution)/shard_map/all_to_all | solution.py:359
  17.8 3.8 %collective-permute-start = (bf16[32,384]{1,0:T(8,128)(2,1)S(1)}, bf16[32,384]{1,0:T(8,128)(2,1)S(1)}, u32[]{:S(2)}, u32[]{:S(2)}) collective-permute-start(bf16[32,384]{1,0:T(8,128)(2,1)S(1)} %pad_maximum_fusion.1), channel_id=1, source_target_pairs={{0,3},{1,0},{2,1},{3,2},{4,7},{5,4},{6,5},{7,6},{8,11},{9,8},{10,9... | collective-permute-start | bytes 73736 | tf_op jit(solution)/shard_map/ppermute | solution.py:356
  20.5 4.5 %collective-permute-start.1 = (bf16[32,384]{1,0:T(8,128)(2,1)S(1)}, bf16[32,384]{1,0:T(8,128)(2,1)S(1)}, u32[]{:S(2)}, u32[]{:S(2)}) collective-permute-start(bf16[32,384]{1,0:T(8,128)(2,1)S(1)} %pad_maximum_fusion.1), channel_id=1, source_target_pairs={{0,2},{1,3},{2,0},{3,1},{4,6},{5,7},{6,4},{7,5},{8,10},{9,11},{10,... | collective-permute-start | bytes 73736 | tf_op jit(solution)/shard_map/ppermute | solution.py:356
  20.8 4.4 %collective-permute-start.2 = (bf16[32,384]{1,0:T(8,128)(2,1)S(1)}, bf16[32,384]{1,0:T(8,128)(2,1)S(1)}, u32[]{:S(2)}, u32[]{:S(2)}) collective-permute-start(bf16[32,384]{1,0:T(8,128)(2,1)S(1)} %pad_maximum_fusion.1), channel_id=1, source_target_pairs={{0,1},{1,2},{2,3},{3,0},{4,5},{5,6},{6,7},{7,4},{8,9},{9,10},{10,1... | collective-permute-start | bytes 73736 | tf_op jit(solution)/shard_map/ppermute | solution.py:356
  53.3 47.9 %all-to-all-start.1 = ((bf16[64,8,1536]{2,1,0:T(8,128)(2,1)}), bf16[64,8,1536]{2,1,0:T(8,128)(2,1)S(1)}, u32[]{:S(2)}, u32[]{:S(2)}) async-start(bf16[64,8,1536]{2,1,0:T(8,128)(2,1)} %bitcast.44), calls=%async_computation.1 | async-start | bytes 3145728 | tf_op jit(solution)/shard_map/all_to_all | solution.py:359
  60.7 18.9 %collective-permute-start.3 = (bf16[256,1408]{1,0:T(8,128)(2,1)}, bf16[256,1408]{1,0:T(8,128)(2,1)}, u32[]{:S(2)}, u32[]{:S(2)}) collective-permute-start(bf16[256,1408]{1,0:T(8,128)(2,1)} %get-tuple-element.31), channel_id=1, source_target_pairs={{0,1},{1,2},{2,3},{3,0},{4,5},{5,6},{6,7},{7,4},{8,9},{9,10},{10,1... | collective-permute-start | bytes 2162696 | tf_op jit(solution)/shard_map/ppermute | solution.py:356
  62.0 17.6 %collective-permute-start.6 = (bf16[256,1408]{1,0:T(8,128)(2,1)}, bf16[256,1408]{1,0:T(8,128)(2,1)}, u32[]{:S(2)}, u32[]{:S(2)}) collective-permute-start(bf16[256,1408]{1,0:T(8,128)(2,1)} %get-tuple-element.30), channel_id=1, source_target_pairs={{0,3},{1,0},{2,1},{3,2},{4,7},{5,4},{6,5},{7,6},{8,11},{9,8},{10,9... | collective-permute-start | bytes 2162696 | tf_op jit(solution)/shard_map/ppermute | solution.py:356
  63.4 31.6 %collective-permute-start.4 = (bf16[256,1408]{1,0:T(8,128)(2,1)}, bf16[256,1408]{1,0:T(8,128)(2,1)}, u32[]{:S(2)}, u32[]{:S(2)}) collective-permute-start(bf16[256,1408]{1,0:T(8,128)(2,1)} %get-tuple-element.30), channel_id=1, source_target_pairs={{0,1},{1,2},{2,3},{3,0},{4,5},{5,6},{6,7},{7,4},{8,9},{9,10},{10,1... | collective-permute-start | bytes 2162696 | tf_op jit(solution)/shard_map/ppermute | solution.py:356
  63.4 31.6 %collective-permute-start.5 = (bf16[256,1408]{1,0:T(8,128)(2,1)}, bf16[256,1408]{1,0:T(8,128)(2,1)}, u32[]{:S(2)}, u32[]{:S(2)}) collective-permute-start(bf16[256,1408]{1,0:T(8,128)(2,1)} %get-tuple-element.31), channel_id=1, source_target_pairs={{0,3},{1,0},{2,1},{3,2},{4,7},{5,4},{6,5},{7,6},{8,11},{9,8},{10,9... | collective-permute-start | bytes 2162696 | tf_op jit(solution)/shard_map/ppermute | solution.py:356
  79.6 30.9 %collective-permute-start.7 = (bf16[256,1408]{1,0:T(8,128)(2,1)}, bf16[256,1408]{1,0:T(8,128)(2,1)}, u32[]{:S(2)}, u32[]{:S(2)}) collective-permute-start(bf16[256,1408]{1,0:T(8,128)(2,1)} %collective-permute-done.3.refs_1_), channel_id=1, source_target_pairs={{0,1},{1,2},{2,3},{3,0},{4,5},{5,6},{6,7},{7,4},{8,9},{9,10},{10,1... | collective-permute-start | bytes 2162696 | tf_op jit(solution)/shard_map/ppermute | solution.py:356
  79.6 30.9 %collective-permute-start.8 = (bf16[256,1408]{1,0:T(8,128)(2,1)}, bf16[256,1408]{1,0:T(8,128)(2,1)}, u32[]{:S(2)}, u32[]{:S(2)}) collective-permute-start(bf16[256,1408]{1,0:T(8,128)(2,1)} %collective-permute-done.6.refs_4_), channel_id=1, source_target_pairs={{0,3},{1,0},{2,1},{3,2},{4,7},{5,4},{6,5},{7,6},{8,11},{9,8},{10,9... | collective-permute-start | bytes 2162696 | tf_op jit(solution)/shard_map/ppermute | solution.py:356
  118.3 64.8 %all-to-all-start.2 = ((bf16[64,8,1536]{2,1,0:T(8,128)(2,1)}), bf16[64,8,1536]{2,1,0:T(8,128)(2,1)}, u32[]{:S(2)}, u32[]{:S(2)}) async-start(bf16[64,8,1536]{2,1,0:T(8,128)(2,1)} %bitcast.45), calls=%async_computation.2 | async-start | bytes 3145728 | tf_op jit(solution)/shard_map/all_to_all | solution.py:359
  129.7 17.7 %collective-permute-start.10 = (bf16[256,1408]{1,0:T(8,128)(2,1)S(1)}, bf16[256,1408]{1,0:T(8,128)(2,1)S(1)}, u32[]{:S(2)}, u32[]{:S(2)}) collective-permute-start(bf16[256,1408]{1,0:T(8,128)(2,1)S(1)} %get-tuple-element.22), channel_id=1, source_target_pairs={{0,3},{1,0},{2,1},{3,2},{4,7},{5,4},{6,5},{7,6},{8,11},{9,8},{10,9... | collective-permute-start | bytes 2162696 | tf_op jit(solution)/shard_map/ppermute | solution.py:356
  132.4 18.2 %collective-permute-start.9 = (bf16[256,1408]{1,0:T(8,128)(2,1)S(1)}, bf16[256,1408]{1,0:T(8,128)(2,1)S(1)}, u32[]{:S(2)}, u32[]{:S(2)}) collective-permute-start(bf16[256,1408]{1,0:T(8,128)(2,1)S(1)} %get-tuple-element.21), channel_id=1, source_target_pairs={{0,1},{1,2},{2,3},{3,0},{4,5},{5,6},{6,7},{7,4},{8,9},{9,10},{10,1... | collective-permute-start | bytes 2162696 | tf_op jit(solution)/shard_map/ppermute | solution.py:356
  135.6 30.4 %collective-permute-start.12 = (bf16[256,1408]{1,0:T(8,128)(2,1)S(1)}, bf16[256,1408]{1,0:T(8,128)(2,1)S(1)}, u32[]{:S(2)}, u32[]{:S(2)}) collective-permute-start(bf16[256,1408]{1,0:T(8,128)(2,1)S(1)} %get-tuple-element.24), channel_id=1, source_target_pairs={{0,1},{1,2},{2,3},{3,0},{4,5},{5,6},{6,7},{7,4},{8,9},{9,10},{10,1... | collective-permute-start | bytes 2162696 | tf_op jit(solution)/shard_map/ppermute | solution.py:356
  135.8 30.2 %collective-permute-start.13 = (bf16[256,1408]{1,0:T(8,128)(2,1)S(1)}, bf16[256,1408]{1,0:T(8,128)(2,1)S(1)}, u32[]{:S(2)}, u32[]{:S(2)}) collective-permute-start(bf16[256,1408]{1,0:T(8,128)(2,1)S(1)} %get-tuple-element.25), channel_id=1, source_target_pairs={{0,3},{1,0},{2,1},{3,2},{4,7},{5,4},{6,5},{7,6},{8,11},{9,8},{10,9... | collective-permute-start | bytes 2162696 | tf_op jit(solution)/shard_map/ppermute | solution.py:356
  153.8 27.6 %collective-permute-start.11 = (bf16[256,1408]{1,0:T(8,128)(2,1)S(1)}, bf16[256,1408]{1,0:T(8,128)(2,1)S(1)}, u32[]{:S(2)}, u32[]{:S(2)}) collective-permute-start(bf16[256,1408]{1,0:T(8,128)(2,1)S(1)} %get-tuple-element.23), channel_id=1, source_target_pairs={{0,1},{1,2},{2,3},{3,0},{4,5},{5,6},{6,7},{7,4},{8,9},{9,10},{10,1... | collective-permute-start | bytes 2162696 | tf_op jit(solution)/shard_map/ppermute | solution.py:356
  153.9 27.5 %collective-permute-start.14 = (bf16[256,1408]{1,0:T(8,128)(2,1)S(1)}, bf16[256,1408]{1,0:T(8,128)(2,1)S(1)}, u32[]{:S(2)}, u32[]{:S(2)}) collective-permute-start(bf16[256,1408]{1,0:T(8,128)(2,1)S(1)} %get-tuple-element.26), channel_id=1, source_target_pairs={{0,3},{1,0},{2,1},{3,2},{4,7},{5,4},{6,5},{7,6},{8,11},{9,8},{10,9... | collective-permute-start | bytes 2162696 | tf_op jit(solution)/shard_map/ppermute | solution.py:356
  183.0 11.7 %copy-start = (s32[16,8]{0,1:T(8,128)S(1)}, s32[16,8]{0,1:T(8,128)}, u32[]{:S(2)}) copy-start(s32[16,8]{0,1:T(8,128)} %param.8) | copy-start | bytes 1540
  183.0 11.8 %copy-start.1 = (f32[16,8]{0,1:T(8,128)S(1)}, f32[16,8]{0,1:T(8,128)}, u32[]{:S(2)}) copy-start(f32[16,8]{0,1:T(8,128)} %param.9) | copy-start | bytes 1540
  183.1 48.7 %all-to-all-start.3 = ((bf16[64,8,1408]{2,1,0:T(8,128)(2,1)}), bf16[64,8,1408]{2,1,0:T(8,128)(2,1)S(1)}, u32[]{:S(2)}, u32[]{:S(2)}) async-start(bf16[64,8,1408]{2,1,0:T(8,128)(2,1)} %bitcast.11), calls=%async_computation.3 | async-start | bytes 2883584 | tf_op jit(solution)/shard_map/all_to_all | solution.py:359
  198.7 4.3 %collective-permute-start.15 = (bf16[32,384]{1,0:T(8,128)(2,1)S(1)}, bf16[32,384]{1,0:T(8,128)(2,1)S(1)}, u32[]{:S(2)}, u32[]{:S(2)}) collective-permute-start(bf16[32,384]{1,0:T(8,128)(2,1)S(1)} %get-tuple-element.34), channel_id=1, source_target_pairs={{0,1},{1,2},{2,3},{3,0},{4,5},{5,6},{6,7},{7,4},{8,9},{9,10},{10,1... | collective-permute-start | bytes 73736 | tf_op jit(solution)/shard_map/ppermute | solution.py:356
  198.8 4.6 %collective-permute-start.16 = (bf16[32,384]{1,0:T(8,128)(2,1)S(1)}, bf16[32,384]{1,0:T(8,128)(2,1)S(1)}, u32[]{:S(2)}, u32[]{:S(2)}) collective-permute-start(bf16[32,384]{1,0:T(8,128)(2,1)S(1)} %get-tuple-element.36), channel_id=1, source_target_pairs={{0,2},{1,3},{2,0},{3,1},{4,6},{5,7},{6,4},{7,5},{8,10},{9,11},{10,... | collective-permute-start | bytes 73736 | tf_op jit(solution)/shard_map/ppermute | solution.py:356
  200.0 3.8 %collective-permute-start.17 = (bf16[32,384]{1,0:T(8,128)(2,1)S(1)}, bf16[32,384]{1,0:T(8,128)(2,1)S(1)}, u32[]{:S(2)}, u32[]{:S(2)}) collective-permute-start(bf16[32,384]{1,0:T(8,128)(2,1)S(1)} %get-tuple-element.35), channel_id=1, source_target_pairs={{0,3},{1,0},{2,1},{3,2},{4,7},{5,4},{6,5},{7,6},{8,11},{9,8},{10,9... | collective-permute-start | bytes 73736 | tf_op jit(solution)/shard_map/ppermute | solution.py:356

commit v4 on v3

--- a/solution.py
+++ b/solution.py
@@ -59,6 +59,10 @@
 
 def forward(x, bufs):
     return dot(x, bufs[0][...]), dot(x, bufs[1][...]), dot_t(x, bufs[2][...])
+
+
+def forward_one(x, bufs, t):
+    return dot_t(x, bufs[2][...]) if t == 2 else dot(x, bufs[t][...])
 
 
 def backward(h, bufs, width):
@@ -216,16 +220,17 @@
             )
             loads.append(weight_loads + x_loads)
         first_load.wait()
-        for i in range(n):
-            done(loads[i])
-            near_loads = [
-                c
-                for k in range(plan.parts)
-                for c in run(plan.copies(me_ref, k, 0, DIRECT, hbm, near, n_sems.at[k], k * DIRECT))
-            ]
+        done(loads[0][3:])
+        for t in range(3):
+            loads[0][t].wait()
+            if t == 2:
+                near_loads = [
+                    c
+                    for k in range(plan.parts)
+                    for c in run(plan.copies(me_ref, k, 0, DIRECT, hbm, near, n_sems.at[k], k * DIRECT))
+                ]
             for j in range(2):
-                for t, term in enumerate(forward(x_buf[2 * i + j], far[3 * i : 3 * i + 3])):
-                    acc[j * half : (j + 1) * half, t * w : (t + 1) * w] += term
+                acc[j * half : (j + 1) * half, t * w : (t + 1) * w] += forward_one(x_buf[j], far, t)
 
         @pl.loop(0, rows // block)
         def _(b):
@@ -285,13 +290,18 @@
     near_cols = plan.parts * DIRECT
 
     def kernel(me_ref, sums_ref, x_hbm, wg, wu, wd, out_ref, x_ref, g, u, d, sems, x_sem):
-        loads = run([pltpu.make_async_copy(x_hbm, x_ref, x_sem.at[0])])
-        for k in range(plan.parts):
-            loads += run(plan.copies(me_ref, k, 0, DIRECT, (wg, wu, wd), (g, u, d), sems.at[k], k * DIRECT))
-        done(loads)
-        for t, term in enumerate(forward(x_ref[...], (g, u, d))):
+        x_load = pltpu.make_async_copy(x_hbm, x_ref, x_sem.at[0])
+        x_load.start()
+        loads = [
+            plan.copies(me_ref, k, 0, DIRECT, (wg, wu, wd), (g, u, d), sems.at[k], k * DIRECT)
+            for k in range(plan.parts)
+        ]
+        by_matrix = [run([c[t] for c in loads]) for t in range(3)]
+        x_load.wait()
+        for t in range(3):
+            done(by_matrix[t])
             c = slice(t * w, (t + 1) * w)
-            out_ref[:, c] = sums_ref[:, c] + term
+            out_ref[:, c] = sums_ref[:, c] + forward_one(x_ref[...], (g, u, d), t)
 
     return call(
         kernel,

time: 234 us -> 235 us (level)
  transfers between devices with their start and end apart: 22 -> 22, of which waited for: 14 -> 14; matrix products, arithmetic and copies ran while one was open for 4% -> 4% of each run, Pallas kernels for 9% -> 10%
where the time goes in v4:
time: 235 us; the launch traced here: 234 us
  waiting for transfers between devices  123 us (52%)
  starting transfers between devices  65.4 us (28%)
  Pallas kernels  33.6 us (14%)
  matrix products  6.02 us (3%)
  local copies, waits for them, and re-layouts  2.83 us (1%)
  other arithmetic  2.51 us (1%)
    ppermute x18, waiting for transfers between devices, shift(): lax.ppermute(v, 'hidden', [(i, (i + k) % parts) for i in range(parts)])  68.4 us
    all_to_all x4, waiting for transfers between devices, exchange(): lax.all_to_all(v.reshape(sources, group, v.shape[1]), 'expert', split_axi...  54.2 us
    all_to_all x4, starting transfers between devices, exchange(): lax.all_to_all(v.reshape(sources, group, v.shape[1]), 'expert', split_axi...  42.2 us
    pallas_call x8, Pallas kernels, call(): pl.pallas_call(kernel, in_specs=specs, out_specs=out_specs or [VMEM] * le...  33.6 us
    ppermute x18, starting transfers between devices, shift(): lax.ppermute(v, 'hidden', [(i, (i + k) % parts) for i in range(parts)])  23.2 us
  transfers between devices with their start and end apart: 22, of which 14 were waited for; matrix products, arithmetic and copies ran while one was open for 4% of the time, Pallas kernels for 10%

profile of v4, /device:TPU:1, one launch (start us, length us, event | category | flops | bytes accessed | tf_op | source)
XLA Modules:
  0.0 233.7 jit_solution(2381728864140304833)
XLA Ops:
  3.3 13.0 %all-to-all-start = ((bf16[64,8,1408]{2,1,0:T(8,128)(2,1)}), bf16[64,8,1408]{2,1,0:T(8,128)(2,1)S(1)}, u32[]{:S(2)}, u32[]{:S(2)}) async-start(bf16[64,8,1408]{2,1,0:T(8,128)(2,1)} %bitcast.2), calls=%async_computation | async-start | bytes 2883584 | tf_op jit(solution)/shard_map/all_to_all | solution.py:369
  17.8 2.7 %collective-permute-start = (bf16[32,384]{1,0:T(8,128)(2,1)S(1)}, bf16[32,384]{1,0:T(8,128)(2,1)S(1)}, u32[]{:S(2)}, u32[]{:S(2)}) collective-permute-start(bf16[32,384]{1,0:T(8,128)(2,1)S(1)} %pad_maximum_fusion.1), channel_id=1, source_target_pairs={{0,3},{1,0},{2,1},{3,2},{4,7},{5,4},{6,5},{7,6},{8,11},{9,8},{10,9... | collective-permute-start | bytes 73736 | tf_op jit(solution)/shard_map/ppermute | solution.py:366
  21.5 3.4 %collective-permute-done.1 = bf16[32,384]{1,0:T(8,128)(2,1)S(1)} collective-permute-done((bf16[32,384]{1,0:T(8,128)(2,1)S(1)}, bf16[32,384]{1,0:T(8,128)(2,1)S(1)}, u32[]{:S(2)}, u32[]{:S(2)}) %collective-permute-start.1) | collective-permute-done | bytes 24608 | tf_op jit(solution)/shard_map/ppermute | solution.py:366
  27.0 26.3 %all-to-all-done = bf16[64,8,1408]{2,1,0:T(8,128)(2,1)S(1)} async-done(((bf16[64,8,1408]{2,1,0:T(8,128)(2,1)}), bf16[64,8,1408]{2,1,0:T(8,128)(2,1)S(1)}, u32[]{:S(2)}, u32[]{:S(2)}) %all-to-all-start) | async-done | bytes 1441824 | tf_op jit(solution)/shard_map/all_to_all | solution.py:369
  53.3 6.1 %all-to-all-start.1 = ((bf16[64,8,1536]{2,1,0:T(8,128)(2,1)}), bf16[64,8,1536]{2,1,0:T(8,128)(2,1)S(1)}, u32[]{:S(2)}, u32[]{:S(2)}) async-start(bf16[64,8,1536]{2,1,0:T(8,128)(2,1)} %bitcast.44), calls=%async_computation.1 | async-start | bytes 3145728 | tf_op jit(solution)/shard_map/all_to_all | solution.py:369
  66.1 13.5 %collective-permute-done.3.refs_1_ = bf16[256,1408]{1,0:T(8,128)(2,1)} collective-permute-done((bf16[256,1408]{1,0:T(8,128)(2,1)}, bf16[256,1408]{1,0:T(8,128)(2,1)}, u32[]{:S(2)}, u32[]{:S(2)}) %collective-permute-start.3) | collective-permute-done | bytes 720928 | tf_op jit(solution)/shard_map/ppermute | solution.py:366
  82.2 3.0 %shard_map.87.refs_0_ = f32[512,768]{1,0:T(8,128)S(1)} custom-call(s32[1]{0:T(128)} %bitcast.1.me_ref, bf16[512,1408]{1,0:T(8,128)(2,1)S(1)} %bitcast.21, bf16[7168,256]{1,0:T(8,128)(2,1)} %bitcast.23, bf16[7168,256]{1,0:T(8,128)(2,1)} %bitcast.30, bf16[256,7168]{1,0:T(8,128)(2,1)} %bitcast.37), custom_call_target="tpu_custom_call" | custom-call | flops 1107296256 | bytes 5636096 | tf_op jit(solution)/shard_map/pallas_call | solution.py:78
  85.2 9.8 %collective-permute-done.4.refs_2_ = bf16[256,1408]{1,0:T(8,128)(2,1)} collective-permute-done((bf16[256,1408]{1,0:T(8,128)(2,1)}, bf16[256,1408]{1,0:T(8,128)(2,1)}, u32[]{:S(2)}, u32[]{:S(2)}) %collective-permute-start.4) | collective-permute-done | bytes 720928 | tf_op jit(solution)/shard_map/ppermute | solution.py:366
  95.0 6.1 %shard_map.88.sums_ref = f32[512,768]{1,0:T(8,128)S(1)} custom-call(s32[1]{0:T(128)} %bitcast.1.me_ref, f32[512,768]{1,0:T(8,128)S(1)} %shard_map.87.refs_0_, bf16[256,1408]{1,0:T(8,128)(2,1)} %collective-permute-done.3.refs_1_, bf16[256,1408]{1,0:T(8,128)(2,1)} %collective-permute-done.4.refs_2_, bf16[256,1408]{1,0:T(8,128)(2,1)} %collective-permute-done.5.refs_3_, ...), custom_call_target="tpu_custom_call" | custom-call | flops 2214592512 | bytes 8650752 | tf_op jit(solution)/shard_map/pallas_call | solution.py:78
  101.1 4.0 %shard_map.89.sums_hbm = f32[512,768]{1,0:T(8,128)S(1)} custom-call(s32[1]{0:T(128)} %bitcast.1.me_ref, f32[512,768]{1,0:T(8,128)S(1)} %shard_map.88.sums_ref, bf16[512,1536]{1,0:T(8,128)(2,1)S(1)} %bitcast.22, bf16[7168,256]{1,0:T(8,128)(2,1)} %bitcast.25, bf16[7168,256]{1,0:T(8,128)(2,1)} %bitcast.32, bf16[256,7168]{1,0:T(8,128)(2,1)} %bitcast.39), custom_call_target="tpu_custom_call" | custom-call | flops 1207959552 | bytes 5767168 | tf_op jit(solution)/shard_map/pallas_call | solution.py:78
  105.1 5.3 %collective-permute-done.7.refs_0_ = bf16[256,1408]{1,0:T(8,128)(2,1)} collective-permute-done((bf16[256,1408]{1,0:T(8,128)(2,1)}, bf16[256,1408]{1,0:T(8,128)(2,1)}, u32[]{:S(2)}, u32[]{:S(2)}) %collective-permute-start.7) | collective-permute-done | bytes 720928 | tf_op jit(solution)/shard_map/ppermute | solution.py:366
  110.5 8.4 %shard_map.90 = (bf16[512,768]{1,0:T(8,128)(2,1)S(1)}, bf16[256,1408]{1,0:T(8,128)(2,1)S(1)}, bf16[256,1408]{1,0:T(8,128)(2,1)S(1)}, bf16[512,1536]{1,0:T(8,128)(2,1)}) custom-call(s32[1]{0:T(128)} %bitcast.1.me_ref, f32[512,768]{1,0:T(8,128)S(1)} %shard_map.89.sums_hbm, bf16[256,1408]{1,0:T(8,128)(2,1)} %collective-permute-done.7.refs_0_, ...), custom_call_target="tpu_custom_call" | custom-call | flops 3422552064 | bytes 4194304 | tf_op jit(solution)/shard_map/pallas_call | solution.py:78
  118.9 11.4 %all-to-all-start.2 = ((bf16[64,8,1536]{2,1,0:T(8,128)(2,1)}), bf16[64,8,1536]{2,1,0:T(8,128)(2,1)}, u32[]{:S(2)}, u32[]{:S(2)}) async-start(bf16[64,8,1536]{2,1,0:T(8,128)(2,1)} %bitcast.45), calls=%async_computation.2 | async-start | bytes 3145728 | tf_op jit(solution)/shard_map/all_to_all | solution.py:369
  130.3 2.7 %collective-permute-start.10 = (bf16[256,1408]{1,0:T(8,128)(2,1)S(1)}, bf16[256,1408]{1,0:T(8,128)(2,1)S(1)}, u32[]{:S(2)}, u32[]{:S(2)}) collective-permute-start(bf16[256,1408]{1,0:T(8,128)(2,1)S(1)} %get-tuple-element.22), channel_id=1, source_target_pairs={{0,3},{1,0},{2,1},{3,2},{4,7},{5,4},{6,5},{7,6},{8,11},{9,8},{10,9... | collective-permute-start | bytes 2162696 | tf_op jit(solution)/shard_map/ppermute | solution.py:366
  133.0 3.2 %shard_map.93 = (bf16[256,1408]{1,0:T(8,128)(2,1)S(1)}, bf16[256,1408]{1,0:T(8,128)(2,1)S(1)}) custom-call(s32[1]{0:T(128)} %bitcast.1.me_ref, bf16[512,768]{1,0:T(8,128)(2,1)S(1)} %get-tuple-element.20.h_ref, bf16[7168,256]{1,0:T(8,128)(2,1)} %bitcast.27, bf16[7168,256]{1,0:T(8,128)(2,1)} %bitcast.34, bf16[256,7168]{1,0:T(8,128)(2,1)} %bitcast.41), custom_call_target="tpu_custom_call" | custom-call | flops 1107296256 | bytes 4980736 | tf_op jit(solution)/shard_map/pallas_call | solution.py:78
  136.4 2.9 %collective-permute-start.13 = (bf16[256,1408]{1,0:T(8,128)(2,1)S(1)}, bf16[256,1408]{1,0:T(8,128)(2,1)S(1)}, u32[]{:S(2)}, u32[]{:S(2)}) collective-permute-start(bf16[256,1408]{1,0:T(8,128)(2,1)S(1)} %get-tuple-element.25), channel_id=1, source_target_pairs={{0,3},{1,0},{2,1},{3,2},{4,7},{5,4},{6,5},{7,6},{8,11},{9,8},{10,9... | collective-permute-start | bytes 2162696 | tf_op jit(solution)/shard_map/ppermute | solution.py:366
  139.3 8.7 %collective-permute-done.10.refs_1_ = bf16[256,1408]{1,0:T(8,128)(2,1)S(1)} collective-permute-done((bf16[256,1408]{1,0:T(8,128)(2,1)S(1)}, bf16[256,1408]{1,0:T(8,128)(2,1)S(1)}, u32[]{:S(2)}, u32[]{:S(2)}) %collective-permute-start.10) | collective-permute-done | bytes 720928 | tf_op jit(solution)/shard_map/ppermute | solution.py:366
  148.0 3.2 %collective-permute-done.9.refs_0_ = bf16[256,1408]{1,0:T(8,128)(2,1)S(1)} collective-permute-done((bf16[256,1408]{1,0:T(8,128)(2,1)S(1)}, bf16[256,1408]{1,0:T(8,128)(2,1)S(1)}, u32[]{:S(2)}, u32[]{:S(2)}) %collective-permute-start.9) | collective-permute-done | bytes 720928 | tf_op jit(solution)/shard_map/ppermute | solution.py:366
  151.2 3.2 %shard_map.92 = (bf16[256,1408]{1,0:T(8,128)(2,1)S(1)}, bf16[256,1408]{1,0:T(8,128)(2,1)S(1)}) custom-call(s32[1]{0:T(128)} %bitcast.1.me_ref, bf16[512,768]{1,0:T(8,128)(2,1)S(1)} %get-tuple-element.20.h_ref, bf16[256,1408]{1,0:T(8,128)(2,1)S(1)} %collective-permute-done.9.refs_0_, bf16[256,1408]{1,0:T(8,128)(2,1)S(1)} %collective-permute-done.10.refs_1_, ...), custom_call_target="tpu_custom_call" | custom-call | flops 1107296256 | bytes 6422528 | tf_op jit(solution)/shard_map/pallas_call | solution.py:78
  157.2 3.0 %shard_map.91 = bf16[512,1408]{1,0:T(8,128)(2,1)S(1)} custom-call(s32[1]{0:T(128)} %bitcast.1.me_ref, bf16[512,768]{1,0:T(8,128)(2,1)S(1)} %get-tuple-element.20.h_ref, bf16[7168,256]{1,0:T(8,128)(2,1)} %bitcast.29, bf16[7168,256]{1,0:T(8,128)(2,1)} %bitcast.36, bf16[256,7168]{1,0:T(8,128)(2,1)} %bitcast.43), custom_call_target="tpu_custom_call" | custom-call | flops 1107296256 | bytes 4980736 | tf_op jit(solution)/shard_map/pallas_call | solution.py:78
  160.2 6.5 %collective-permute-done.12 = bf16[256,1408]{1,0:T(8,128)(2,1)S(1)} collective-permute-done((bf16[256,1408]{1,0:T(8,128)(2,1)S(1)}, bf16[256,1408]{1,0:T(8,128)(2,1)S(1)}, u32[]{:S(2)}, u32[]{:S(2)}) %collective-permute-start.12) | collective-permute-done | bytes 720928 | tf_op jit(solution)/shard_map/ppermute | solution.py:366
  166.6 15.3 %collective-permute-done.11 = bf16[256,1408]{1,0:T(8,128)(2,1)S(1)} collective-permute-done((bf16[256,1408]{1,0:T(8,128)(2,1)S(1)}, bf16[256,1408]{1,0:T(8,128)(2,1)S(1)}, u32[]{:S(2)}, u32[]{:S(2)}) %collective-permute-start.11) | collective-permute-done | bytes 720928 | tf_op jit(solution)/shard_map/ppermute | solution.py:366
  183.6 11.7 %all-to-all-start.3 = ((bf16[64,8,1408]{2,1,0:T(8,128)(2,1)}), bf16[64,8,1408]{2,1,0:T(8,128)(2,1)S(1)}, u32[]{:S(2)}, u32[]{:S(2)}) async-start(bf16[64,8,1408]{2,1,0:T(8,128)(2,1)} %bitcast.11), calls=%async_computation.3 | async-start | bytes 2883584 | tf_op jit(solution)/shard_map/all_to_all | solution.py:369
  204.4 27.9 %all-to-all-done.3 = bf16[64,8,1408]{2,1,0:T(8,128)(2,1)S(1)} async-done(((bf16[64,8,1408]{2,1,0:T(8,128)(2,1)}), bf16[64,8,1408]{2,1,0:T(8,128)(2,1)S(1)}, u32[]{:S(2)}, u32[]{:S(2)}) %all-to-all-start.3) | async-done | bytes 1441824 | tf_op jit(solution)/shard_map/all_to_all | solution.py:369
  (51 shorter events, 31.5 us)
Async XLA Ops:
  3.3 49.9 %all-to-all-start = ((bf16[64,8,1408]{2,1,0:T(8,128)(2,1)}), bf16[64,8,1408]{2,1,0:T(8,128)(2,1)S(1)}, u32[]{:S(2)}, u32[]{:S(2)}) async-start(bf16[64,8,1408]{2,1,0:T(8,128)(2,1)} %bitcast.2), calls=%async_computation | async-start | bytes 2883584 | tf_op jit(solution)/shard_map/all_to_all | solution.py:369
  17.8 3.8 %collective-permute-start = (bf16[32,384]{1,0:T(8,128)(2,1)S(1)}, bf16[32,384]{1,0:T(8,128)(2,1)S(1)}, u32[]{:S(2)}, u32[]{:S(2)}) collective-permute-start(bf16[32,384]{1,0:T(8,128)(2,1)S(1)} %pad_maximum_fusion.1), channel_id=1, source_target_pairs={{0,3},{1,0},{2,1},{3,2},{4,7},{5,4},{6,5},{7,6},{8,11},{9,8},{10,9... | collective-permute-start | bytes 73736 | tf_op jit(solution)/shard_map/ppermute | solution.py:366
  20.5 4.5 %collective-permute-start.1 = (bf16[32,384]{1,0:T(8,128)(2,1)S(1)}, bf16[32,384]{1,0:T(8,128)(2,1)S(1)}, u32[]{:S(2)}, u32[]{:S(2)}) collective-permute-start(bf16[32,384]{1,0:T(8,128)(2,1)S(1)} %pad_maximum_fusion.1), channel_id=1, source_target_pairs={{0,2},{1,3},{2,0},{3,1},{4,6},{5,7},{6,4},{7,5},{8,10},{9,11},{10,... | collective-permute-start | bytes 73736 | tf_op jit(solution)/shard_map/ppermute | solution.py:366
  20.8 4.4 %collective-permute-start.2 = (bf16[32,384]{1,0:T(8,128)(2,1)S(1)}, bf16[32,384]{1,0:T(8,128)(2,1)S(1)}, u32[]{:S(2)}, u32[]{:S(2)}) collective-permute-start(bf16[32,384]{1,0:T(8,128)(2,1)S(1)} %pad_maximum_fusion.1), channel_id=1, source_target_pairs={{0,1},{1,2},{2,3},{3,0},{4,5},{5,6},{6,7},{7,4},{8,9},{9,10},{10,1... | collective-permute-start | bytes 73736 | tf_op jit(solution)/shard_map/ppermute | solution.py:366
  53.3 47.9 %all-to-all-start.1 = ((bf16[64,8,1536]{2,1,0:T(8,128)(2,1)}), bf16[64,8,1536]{2,1,0:T(8,128)(2,1)S(1)}, u32[]{:S(2)}, u32[]{:S(2)}) async-start(bf16[64,8,1536]{2,1,0:T(8,128)(2,1)} %bitcast.44), calls=%async_computation.1 | async-start | bytes 3145728 | tf_op jit(solution)/shard_map/all_to_all | solution.py:369
  60.7 18.9 %collective-permute-start.3 = (bf16[256,1408]{1,0:T(8,128)(2,1)}, bf16[256,1408]{1,0:T(8,128)(2,1)}, u32[]{:S(2)}, u32[]{:S(2)}) collective-permute-start(bf16[256,1408]{1,0:T(8,128)(2,1)} %get-tuple-element.31), channel_id=1, source_target_pairs={{0,1},{1,2},{2,3},{3,0},{4,5},{5,6},{6,7},{7,4},{8,9},{9,10},{10,1... | collective-permute-start | bytes 2162696 | tf_op jit(solution)/shard_map/ppermute | solution.py:366
  62.0 17.6 %collective-permute-start.6 = (bf16[256,1408]{1,0:T(8,128)(2,1)}, bf16[256,1408]{1,0:T(8,128)(2,1)}, u32[]{:S(2)}, u32[]{:S(2)}) collective-permute-start(bf16[256,1408]{1,0:T(8,128)(2,1)} %get-tuple-element.30), channel_id=1, source_target_pairs={{0,3},{1,0},{2,1},{3,2},{4,7},{5,4},{6,5},{7,6},{8,11},{9,8},{10,9... | collective-permute-start | bytes 2162696 | tf_op jit(solution)/shard_map/ppermute | solution.py:366
  63.4 31.6 %collective-permute-start.4 = (bf16[256,1408]{1,0:T(8,128)(2,1)}, bf16[256,1408]{1,0:T(8,128)(2,1)}, u32[]{:S(2)}, u32[]{:S(2)}) collective-permute-start(bf16[256,1408]{1,0:T(8,128)(2,1)} %get-tuple-element.30), channel_id=1, source_target_pairs={{0,1},{1,2},{2,3},{3,0},{4,5},{5,6},{6,7},{7,4},{8,9},{9,10},{10,1... | collective-permute-start | bytes 2162696 | tf_op jit(solution)/shard_map/ppermute | solution.py:366
  63.4 31.6 %collective-permute-start.5 = (bf16[256,1408]{1,0:T(8,128)(2,1)}, bf16[256,1408]{1,0:T(8,128)(2,1)}, u32[]{:S(2)}, u32[]{:S(2)}) collective-permute-start(bf16[256,1408]{1,0:T(8,128)(2,1)} %get-tuple-element.31), channel_id=1, source_target_pairs={{0,3},{1,0},{2,1},{3,2},{4,7},{5,4},{6,5},{7,6},{8,11},{9,8},{10,9... | collective-permute-start | bytes 2162696 | tf_op jit(solution)/shard_map/ppermute | solution.py:366
  79.6 30.9 %collective-permute-start.7 = (bf16[256,1408]{1,0:T(8,128)(2,1)}, bf16[256,1408]{1,0:T(8,128)(2,1)}, u32[]{:S(2)}, u32[]{:S(2)}) collective-permute-start(bf16[256,1408]{1,0:T(8,128)(2,1)} %collective-permute-done.3.refs_1_), channel_id=1, source_target_pairs={{0,1},{1,2},{2,3},{3,0},{4,5},{5,6},{6,7},{7,4},{8,9},{9,10},{10,1... | collective-permute-start | bytes 2162696 | tf_op jit(solution)/shard_map/ppermute | solution.py:366
  79.6 30.9 %collective-permute-start.8 = (bf16[256,1408]{1,0:T(8,128)(2,1)}, bf16[256,1408]{1,0:T(8,128)(2,1)}, u32[]{:S(2)}, u32[]{:S(2)}) collective-permute-start(bf16[256,1408]{1,0:T(8,128)(2,1)} %collective-permute-done.6.refs_4_), channel_id=1, source_target_pairs={{0,3},{1,0},{2,1},{3,2},{4,7},{5,4},{6,5},{7,6},{8,11},{9,8},{10,9... | collective-permute-start | bytes 2162696 | tf_op jit(solution)/shard_map/ppermute | solution.py:366
  118.9 64.8 %all-to-all-start.2 = ((bf16[64,8,1536]{2,1,0:T(8,128)(2,1)}), bf16[64,8,1536]{2,1,0:T(8,128)(2,1)}, u32[]{:S(2)}, u32[]{:S(2)}) async-start(bf16[64,8,1536]{2,1,0:T(8,128)(2,1)} %bitcast.45), calls=%async_computation.2 | async-start | bytes 3145728 | tf_op jit(solution)/shard_map/all_to_all | solution.py:369
  130.3 17.7 %collective-permute-start.10 = (bf16[256,1408]{1,0:T(8,128)(2,1)S(1)}, bf16[256,1408]{1,0:T(8,128)(2,1)S(1)}, u32[]{:S(2)}, u32[]{:S(2)}) collective-permute-start(bf16[256,1408]{1,0:T(8,128)(2,1)S(1)} %get-tuple-element.22), channel_id=1, source_target_pairs={{0,3},{1,0},{2,1},{3,2},{4,7},{5,4},{6,5},{7,6},{8,11},{9,8},{10,9... | collective-permute-start | bytes 2162696 | tf_op jit(solution)/shard_map/ppermute | solution.py:366
  133.0 18.2 %collective-permute-start.9 = (bf16[256,1408]{1,0:T(8,128)(2,1)S(1)}, bf16[256,1408]{1,0:T(8,128)(2,1)S(1)}, u32[]{:S(2)}, u32[]{:S(2)}) collective-permute-start(bf16[256,1408]{1,0:T(8,128)(2,1)S(1)} %get-tuple-element.21), channel_id=1, source_target_pairs={{0,1},{1,2},{2,3},{3,0},{4,5},{5,6},{6,7},{7,4},{8,9},{9,10},{10,1... | collective-permute-start | bytes 2162696 | tf_op jit(solution)/shard_map/ppermute | solution.py:366
  136.2 30.4 %collective-permute-start.12 = (bf16[256,1408]{1,0:T(8,128)(2,1)S(1)}, bf16[256,1408]{1,0:T(8,128)(2,1)S(1)}, u32[]{:S(2)}, u32[]{:S(2)}) collective-permute-start(bf16[256,1408]{1,0:T(8,128)(2,1)S(1)} %get-tuple-element.24), channel_id=1, source_target_pairs={{0,1},{1,2},{2,3},{3,0},{4,5},{5,6},{6,7},{7,4},{8,9},{9,10},{10,1... | collective-permute-start | bytes 2162696 | tf_op jit(solution)/shard_map/ppermute | solution.py:366
  136.4 30.2 %collective-permute-start.13 = (bf16[256,1408]{1,0:T(8,128)(2,1)S(1)}, bf16[256,1408]{1,0:T(8,128)(2,1)S(1)}, u32[]{:S(2)}, u32[]{:S(2)}) collective-permute-start(bf16[256,1408]{1,0:T(8,128)(2,1)S(1)} %get-tuple-element.25), channel_id=1, source_target_pairs={{0,3},{1,0},{2,1},{3,2},{4,7},{5,4},{6,5},{7,6},{8,11},{9,8},{10,9... | collective-permute-start | bytes 2162696 | tf_op jit(solution)/shard_map/ppermute | solution.py:366
  154.4 27.6 %collective-permute-start.11 = (bf16[256,1408]{1,0:T(8,128)(2,1)S(1)}, bf16[256,1408]{1,0:T(8,128)(2,1)S(1)}, u32[]{:S(2)}, u32[]{:S(2)}) collective-permute-start(bf16[256,1408]{1,0:T(8,128)(2,1)S(1)} %get-tuple-element.23), channel_id=1, source_target_pairs={{0,1},{1,2},{2,3},{3,0},{4,5},{5,6},{6,7},{7,4},{8,9},{9,10},{10,1... | collective-permute-start | bytes 2162696 | tf_op jit(solution)/shard_map/ppermute | solution.py:366
  154.5 27.5 %collective-permute-start.14 = (bf16[256,1408]{1,0:T(8,128)(2,1)S(1)}, bf16[256,1408]{1,0:T(8,128)(2,1)S(1)}, u32[]{:S(2)}, u32[]{:S(2)}) collective-permute-start(bf16[256,1408]{1,0:T(8,128)(2,1)S(1)} %get-tuple-element.26), channel_id=1, source_target_pairs={{0,3},{1,0},{2,1},{3,2},{4,7},{5,4},{6,5},{7,6},{8,11},{9,8},{10,9... | collective-permute-start | bytes 2162696 | tf_op jit(solution)/shard_map/ppermute | solution.py:366
  183.6 11.7 %copy-start = (s32[16,8]{0,1:T(8,128)S(1)}, s32[16,8]{0,1:T(8,128)}, u32[]{:S(2)}) copy-start(s32[16,8]{0,1:T(8,128)} %param.8) | copy-start | bytes 1540
  183.6 11.8 %copy-start.1 = (f32[16,8]{0,1:T(8,128)S(1)}, f32[16,8]{0,1:T(8,128)}, u32[]{:S(2)}) copy-start(f32[16,8]{0,1:T(8,128)} %param.9) | copy-start | bytes 1540
  183.6 48.7 %all-to-all-start.3 = ((bf16[64,8,1408]{2,1,0:T(8,128)(2,1)}), bf16[64,8,1408]{2,1,0:T(8,128)(2,1)S(1)}, u32[]{:S(2)}, u32[]{:S(2)}) async-start(bf16[64,8,1408]{2,1,0:T(8,128)(2,1)} %bitcast.11), calls=%async_computation.3 | async-start | bytes 2883584 | tf_op jit(solution)/shard_map/all_to_all | solution.py:369
  199.3 4.3 %collective-permute-start.15 = (bf16[32,384]{1,0:T(8,128)(2,1)S(1)}, bf16[32,384]{1,0:T(8,128)(2,1)S(1)}, u32[]{:S(2)}, u32[]{:S(2)}) collective-permute-start(bf16[32,384]{1,0:T(8,128)(2,1)S(1)} %get-tuple-element.34), channel_id=1, source_target_pairs={{0,1},{1,2},{2,3},{3,0},{4,5},{5,6},{6,7},{7,4},{8,9},{9,10},{10,1... | collective-permute-start | bytes 73736 | tf_op jit(solution)/shard_map/ppermute | solution.py:366
  199.4 4.6 %collective-permute-start.16 = (bf16[32,384]{1,0:T(8,128)(2,1)S(1)}, bf16[32,384]{1,0:T(8,128)(2,1)S(1)}, u32[]{:S(2)}, u32[]{:S(2)}) collective-permute-start(bf16[32,384]{1,0:T(8,128)(2,1)S(1)} %get-tuple-element.36), channel_id=1, source_target_pairs={{0,2},{1,3},{2,0},{3,1},{4,6},{5,7},{6,4},{7,5},{8,10},{9,11},{10,... | collective-permute-start | bytes 73736 | tf_op jit(solution)/shard_map/ppermute | solution.py:366
  200.6 3.8 %collective-permute-start.17 = (bf16[32,384]{1,0:T(8,128)(2,1)S(1)}, bf16[32,384]{1,0:T(8,128)(2,1)S(1)}, u32[]{:S(2)}, u32[]{:S(2)}) collective-permute-start(bf16[32,384]{1,0:T(8,128)(2,1)S(1)} %get-tuple-element.35), channel_id=1, source_target_pairs={{0,3},{1,0},{2,1},{3,2},{4,7},{5,4},{6,5},{7,6},{8,11},{9,8},{10,9... | collective-permute-start | bytes 73736 | tf_op jit(solution)/shard_map/ppermute | solution.py:366
